TPU v7x, 512 devices: a whole 4x4x16 slice. The times are simulated.
512 devices in a mesh: rows: 16 (over z), cols: 32 (over x, y, core).
Axes of the slice: x: 4, y: 4, z: 16, core: 2. Of those that a mesh axis runs over, the one named last changes fastest.
Arguments:
- boundary_in: bfloat16 [16, 32, 16, 256, 256], P('rows', 'cols'), may hold values from -6 to 6
- row_operator: bfloat16 [16, 32, 16, 16], P('rows', 'cols'), may hold values from -1.5 to 1.5
- charges: int32 [16, 32], P('rows', 'cols'), may hold values from 64 to 192
Outputs:
- boundary_out: bfloat16 [16, 32, 16, 256, 256], P('rows', 'cols')
- operator_grad: float32 [16, 32, 16, 16], P('rows', 'cols')
All inputs are finite; a program needn't handle non-finite values.
Results may differ from a plain program's by a relative error of at most 0.005.
Values may be sent and summed in bfloat16 or wider, within the bound.
A program may use at most 64 MiB of HBM per device.

v0:
```python
import math

import jax
import jax.numpy as jnp
from jax import lax
from jax.sharding import PartitionSpec as P


def prefix(part, axis, combine, identity):
    place = lax.axis_index(axis)
    gathered = lax.all_gather(part, axis)
    state = jnp.zeros_like(part) + jnp.asarray(identity, part.dtype)

    def one(lap, state):
        return combine(state, lax.dynamic_index_in_dim(gathered, lap, 0, False))

    return lax.fori_loop(0, place, one, state)


def from_root(array, axis, root):
    mine = lax.axis_index(axis) == root
    return lax.psum(jnp.where(mine, array, jnp.zeros_like(array)), axis)


def from_behind(value, axis, steps):
    count = lax.axis_size(axis)
    first, last = (max(0, -steps), min(count, count - steps))
    return lax.ppermute(value, axis, [(source, source + steps) for source in range(first, last)])


def keep_mask(charge_row, phys_dim, bond_dim):
    phys_odd = jnp.arange(phys_dim) >= phys_dim // 2
    left_odd = jnp.arange(bond_dim)[None, :] >= charge_row[:, None]
    right_odd = jnp.arange(bond_dim) >= bond_dim // 2
    parity = jnp.logical_xor(
        jnp.logical_xor(phys_odd[None, :, None, None], left_odd[:, None, :, None]),
        right_odd[None, None, None, :],
    )
    return jnp.logical_not(parity)


def add_grams(first, second):
    return first + second


def inner_cols(left_flat, right_flat):
    return lax.dot_general(
        left_flat, right_flat, (((0,), (0,)), ((), ())), preferred_element_type=jnp.float32
    )


def shards(boundary_in, row_operator, charges):
    site_count = boundary_in.shape[1]
    phys_dim = boundary_in.shape[2]
    bond_dim = boundary_in.shape[4]
    col_groups = lax.axis_size("cols")
    all_sites = site_count * col_groups
    applied = jnp.einsum(
        "spq,sqlc->splc", row_operator[0], boundary_in[0], preferred_element_type=jnp.float32
    )
    applied = jnp.where(keep_mask(charges[0], phys_dim, bond_dim), applied, 0.0).astype(
        jnp.bfloat16
    )
    flat_rows = applied.reshape(-1, bond_dim)
    local_gram = inner_cols(flat_rows, flat_rows) / (all_sites * phys_dim * bond_dim / 2.0)
    before = prefix(local_gram, "cols", add_grams, jnp.zeros_like(local_gram))
    running = before + local_gram
    whole_gram = from_root(running, "cols", col_groups - 1)
    factor = jnp.linalg.cholesky(whole_gram)
    inverse = jax.scipy.linalg.solve_triangular(
        factor, jnp.eye(bond_dim, dtype=jnp.float32), lower=True
    )
    compressed = jnp.dot(
        flat_rows, inverse.T, precision=lax.Precision.HIGHEST, preferred_element_type=jnp.float32
    )
    compressed = compressed.astype(jnp.bfloat16)
    from_above = from_behind(compressed, "rows", 1)
    mix_scale = 2.0 / (bond_dim * math.sqrt(all_sites * phys_dim))
    correlation = lax.psum(inner_cols(from_above, compressed), "cols")
    correlation = (correlation * mix_scale).astype(jnp.bfloat16)
    adjoint = jnp.dot(compressed, correlation.T, preferred_element_type=jnp.float32).astype(
        jnp.bfloat16
    )
    adjoint = from_behind(adjoint, "rows", -1)
    adjoint = adjoint.reshape(site_count, phys_dim, bond_dim, bond_dim)
    gradient = (
        jnp.einsum("splc,sqlc->spq", adjoint, boundary_in[0], preferred_element_type=jnp.float32)
        / bond_dim
    )
    boundary_out = compressed.reshape(site_count, phys_dim, bond_dim, bond_dim)
    return (boundary_out[None], gradient[None])


def solution(mesh):
    return jax.shard_map(
        shards,
        mesh=mesh,
        in_specs=(
            P("rows", "cols", None, None, None),
            P("rows", "cols", None, None),
            P("rows", "cols"),
        ),
        out_specs=(P("rows", "cols", None, None, None), P("rows", "cols", None, None)),
        check_vma=False,
    )
```

profile of v0, /device:TPU:1, one launch (start us, length us, event | category | flops | bytes accessed | tf_op | source)
XLA Modules:
  0.0 582.9 jit_solution(5288608303625841610)
XLA Ops:
  7.2 0.0 all-gather.3.cloned.1.call-start
  7.9 0.1 broadcast_xor_fusion
  8.0 3.2 select_convert_fusion
  11.2 1.7 fusion.1
  12.9 0.0 all-reduce.4.cloned.1.call-start
  13.0 80.7 %all-gather.3.cloned.1.call-done = f32[8192,256]{0,1:T(8,128)} async-done(((f32[256,256]{0,1:T(8,128)}), f32[8192,256]{0,1:T(8,128)}) %all-gather.3.cloned.1.call-update) | async-done | bytes 8388624 | tf_op jit(solution)/shard_map/all_gather | solution.py:11
  93.6 9.0 %copy.38 = f32[8192,256]{1,0:T(8,128)} copy(f32[8192,256]{0,1:T(8,128)} %all-gather.3.cloned.1.call-done) | data formatting | bytes 16777216 | tf_op jit(solution)/shard_map/while | solution.py:17
  102.6 1.1 while.11
  102.7 1.0 bitcast_add_fusion.3
  103.7 0.1 copy.26
  103.9 0.7 add_select_fusion
  104.6 0.2 all-reduce.6.cloned.1.call-start
  104.9 2.1 copy.20
  107.0 159.4 %all-reduce.4.cloned.1.call-done = f32[256,256]{0,1:T(8,128)} async-done(((f32[256,256]{0,1:T(8,128)}), f32[256,256]{0,1:T(8,128)}) %all-reduce.4.cloned.1.call-update) | async-done | bytes 262160 | tf_op jit(solution)/shard_map/psum | solution.py:22
  266.3 1.1 copy.27
  267.4 1.0 fusion.7
  268.4 11.7 %cholesky.49 = f32[128,128]{1,0:T(8,128)S(1)} custom-call(f32[128,128]{1,0:T(8,128)S(1)} %cholesky.115), custom_call_target="Cholesky" | custom-call | tf_op jit(solution)/shard_map/jit(cholesky)/cholesky | solution.py:69
  280.2 9.8 %custom-call.15 = f32[1,128,128]{1,2,0:T(8,128)S(1)} custom-call(f32[1,128,128]{2,1,0:T(8,128)S(1)} %get-tuple-element.69), custom_call_target="InvertDiagBlocksLowerTriangular" | custom-call | tf_op jit(solution)/shard_map/jit(cholesky)/cholesky | solution.py:69
  290.0 0.2 fusion.13
  290.2 0.3 convolution_subtract_fusion.1
  290.5 11.7 %cholesky.103 = f32[128,128]{1,0:T(8,128)S(1)} custom-call(f32[128,128]{1,0:T(8,128)S(1)} %convolution_subtract_fusion.1), custom_call_target="Cholesky" | custom-call | tf_op jit(solution)/shard_map/jit(cholesky)/cholesky | solution.py:69
  302.2 0.1 copy.30
  302.3 0.1 copy.29
  302.4 0.1 copy.28
  302.6 0.7 compare_reduce_fusion
  304.6 0.1 triangular_solve.63
  304.7 4.4 while.12
  304.9 0.6 fusion.34
  305.5 1.4 dynamic-slice.7
  306.8 0.1 copy.46
  307.0 0.6 fusion.34
  307.6 1.4 dynamic-slice.7
  309.0 0.1 copy.46
  309.1 19.7 %custom-call.16 = f32[2,128,128]{1,2,0:T(8,128)S(1)} custom-call(f32[2,128,128]{2,1,0:T(8,128)S(1)} %get-tuple-element.33), custom_call_target="InvertDiagBlocksLowerTriangular" | custom-call | tf_op jit(solution)/shard_map/jit(_solve_triangular)/triangular_solve | solution.py:70
  328.8 0.3 fusion.9
  329.0 0.3 convolution_subtract_fusion
  329.4 0.3 fusion.12
  329.7 3.4 convolution_convert_fusion.1
  333.1 3.3 collective-permute-start
  336.5 44.0 %collective-permute-done = bf16[4096,256]{1,0:T(8,128)(2,1)S(1)} collective-permute-done((bf16[4096,256]{1,0:T(8,128)(2,1)S(1)}, bf16[4096,256]{1,0:T(8,128)(2,1)S(1)}, u32[]{:S(2)}, u32[]{:S(2)}) %collective-permute-start) | collective-permute-done | bytes 2097184 | tf_op jit(solution)/shard_map/ppermute | solution.py:28
  380.5 1.4 fusion.20
  381.9 135.3 %all-reduce.6.cloned.1.call-done = f32[256,256]{1,0:T(8,128)} async-done(((f32[256,256]{1,0:T(8,128)}), f32[256,256]{1,0:T(8,128)}) %all-reduce.6.cloned.1.call-update) | async-done | bytes 262160 | tf_op jit(solution)/shard_map/psum | solution.py:79
  517.2 3.0 convolution_convert_fusion
  520.2 1.3 collective-permute-start.1
  521.5 3.3 copy.33
  524.8 43.9 %collective-permute-done.1 = bf16[4096,256]{1,0:T(8,128)(2,1)} collective-permute-done((bf16[4096,256]{1,0:T(8,128)(2,1)}, bf16[4096,256]{1,0:T(8,128)(2,1)}, u32[]{:S(2)}, u32[]{:S(2)}) %collective-permute-start.1) | collective-permute-done | bytes 2097184 | tf_op jit(solution)/shard_map/ppermute | solution.py:28
  568.7 4.5 copy.32
  573.3 3.2 fusion.3
  (27 shorter events, 0.3 us)
Async XLA Ops:
  7.2 0.9 copy-start
  7.2 86.4 %all-gather.3.cloned.1.call-start = ((), (), s32[]{:S(2)}) async-start(), calls=%async_computation.2 | async-start | bytes 8650752 | tf_op jit(solution)/shard_map/all_gather | solution.py:11
  12.9 253.4 %all-reduce.4.cloned.1.call-start = ((), (), s32[]{:S(2)}) async-start(), calls=%async_computation | async-start | bytes 524288 | tf_op jit(solution)/shard_map/psum | solution.py:22
  102.6 1.2 copy-start.2
  104.6 412.5 %all-reduce.6.cloned.1.call-start = ((), (), s32[]{:S(2)}) async-start(), calls=%async_computation.1 | async-start | bytes 524288 | tf_op jit(solution)/shard_map/psum | solution.py:79
  333.1 184.0 %copy-start.1 = (bf16[4096,256]{1,0:T(8,128)(2,1)}, bf16[4096,256]{1,0:T(8,128)(2,1)S(1)}, u32[]{:S(2)}) copy-start(bf16[4096,256]{1,0:T(8,128)(2,1)S(1)} %convolution_convert_fusion.1) | copy-start | bytes 6291460
  333.1 47.3 %collective-permute-start = (bf16[4096,256]{1,0:T(8,128)(2,1)S(1)}, bf16[4096,256]{1,0:T(8,128)(2,1)S(1)}, u32[]{:S(2)}, u32[]{:S(2)}) collective-permute-start(bf16[4096,256]{1,0:T(8,128)(2,1)S(1)} %convolution_convert_fusion.1), channel_id=1, source_target_pairs={{0,32},{32,64},{64,96},{96,128},{128,160},{160,192},{192,224},{224... | collective-permute-start | bytes 6291464 | tf_op jit(solution)/shard_map/ppermute | solution.py:28
  520.2 48.5 %collective-permute-start.1 = (bf16[4096,256]{1,0:T(8,128)(2,1)}, bf16[4096,256]{1,0:T(8,128)(2,1)}, u32[]{:S(2)}, u32[]{:S(2)}) collective-permute-start(bf16[4096,256]{1,0:T(8,128)(2,1)} %convolution_convert_fusion), channel_id=1, source_target_pairs={{32,0},{64,32},{96,64},{128,96},{160,128},{192,160},{224,192},{256... | collective-permute-start | bytes 6291464 | tf_op jit(solution)/shard_map/ppermute | solution.py:28
Sparse Core Ops, SparseCore 0:
  13.0 80.5 all-gather.2
  104.8 161.5 all-reduce.3
  382.0 135.0 all-reduce.5
where the time goes:
time: 585 us; the launch traced here: 583 us
  waiting for transfers between devices  463 us (79%)
  other arithmetic  56.6 us (10%)
  local copies, waits for them, and re-layouts  24.7 us (4%)
  matrix products  17.3 us (3%)
  between operations  15.9 us (3%)
    psum x1, waiting for transfers between devices, from_root(): return lax.psum(jnp.where(mine, array, jnp.zeros_like(array)), axis)  159 us
    psum x1, waiting for transfers between devices, shards(): correlation = lax.psum(inner_cols(from_above, compressed), 'cols')  135 us
    ppermute x2, waiting for transfers between devices, from_behind(): lax.ppermute(value, axis, [(source, source + steps) for source in range(f...  87.9 us
    all_gather x1, waiting for transfers between devices, prefix(): gathered = lax.all_gather(part, axis)  80.7 us
    another operation x6, other arithmetic, shards(): factor = jnp.linalg.cholesky(whole_gram)  34 us
    another operation x3, other arithmetic, shards(): jax.scipy.linalg.solve_triangular(factor, jnp.eye(bond_dim, dtype=jnp.flo...  19.7 us
    another operation x13, local copies, waits for them, and re-layouts  12 us
  transfers between devices with their start and end apart: 5, of which 5 were waited for; matrix products, arithmetic and copies ran while one was open for 1% of the time, Pallas kernels for 0%

commit v1 on v0

v1 whole, which is shorter than its diff:
```python
import functools
import math

import jax
import jax.numpy as jnp
from jax import lax
from jax.experimental import pallas as pl
from jax.experimental.pallas import tpu as pltpu
from jax.sharding import PartitionSpec as P

HIGH = lax.Precision.HIGHEST
MESH = pl.DeviceIdType.MESH


def from_next(value):
    count = lax.axis_size("rows")
    return lax.ppermute(value, "rows", [(r + 1, r) for r in range(count - 1)])


def sum_kernel(count, part_ref, out_ref, landed, whole, send_a, recv_a, send_b, recv_b):
    me = lax.axis_index("cols")

    def after(k):
        return lax.rem(me + k, count)

    def before(k):
        return lax.rem(me + count - k, count)

    barrier = pltpu.get_barrier_semaphore()

    @pl.loop(1, count)
    def _(k):
        pl.semaphore_signal(barrier, inc=1, device_id={"cols": after(k)}, device_id_type=MESH)

    pl.semaphore_wait(barrier, count - 1)

    def scatter(k):
        return pltpu.make_async_remote_copy(
            src_ref=part_ref.at[after(k)],
            dst_ref=landed.at[k],
            send_sem=send_a.at[k],
            recv_sem=recv_a.at[k],
            device_id={"cols": after(k)},
            device_id_type=MESH,
        )

    @pl.loop(1, count)
    def _(k):
        scatter(k).start()

    landed[0] = part_ref[me]

    @pl.loop(1, count)
    def _(k):
        scatter(k).wait_recv()

    whole[me] = jnp.sum(landed[...], axis=0)

    def gather(k, owner):
        return pltpu.make_async_remote_copy(
            src_ref=whole.at[owner],
            dst_ref=whole.at[owner],
            send_sem=send_b.at[k],
            recv_sem=recv_b.at[k],
            device_id={"cols": after(k)},
            device_id_type=MESH,
        )

    @pl.loop(1, count)
    def _(k):
        gather(k, me).start()

    @pl.loop(1, count)
    def _(k):
        gather(k, before(k)).wait_recv()

    out_ref[...] = whole[...]

    @pl.loop(1, count)
    def _(k):
        scatter(k).wait_send()
        gather(k, me).wait_send()


def sum_over_cols(part, collective_id):
    count = lax.axis_size("cols")
    shape = part.shape
    pieces = (count, part.size // count // 128, 128)
    total = pl.pallas_call(
        functools.partial(sum_kernel, count),
        out_shape=jax.ShapeDtypeStruct(pieces, jnp.float32),
        in_specs=[pl.BlockSpec(memory_space=pltpu.VMEM)],
        out_specs=pl.BlockSpec(memory_space=pltpu.VMEM),
        scratch_shapes=[
            pltpu.VMEM(pieces, jnp.float32),
            pltpu.VMEM(pieces, jnp.float32),
            pltpu.SemaphoreType.DMA((count,)),
            pltpu.SemaphoreType.DMA((count,)),
            pltpu.SemaphoreType.DMA((count,)),
            pltpu.SemaphoreType.DMA((count,)),
        ],
        compiler_params=pltpu.CompilerParams(collective_id=collective_id, has_side_effects=True),
        cost_estimate=pl.CostEstimate(flops=part.size, bytes_accessed=16 * part.size, transcendentals=0),
        name="sum_over_cols",
    )(part.reshape(pieces))
    return total.reshape(shape)


def odd_rows(charge, phys_dim, bond_dim):
    phys_odd = jnp.arange(phys_dim) >= phys_dim // 2
    left_odd = jnp.arange(bond_dim) >= charge
    return jnp.logical_xor(phys_odd[:, None], left_odd[None, :]).reshape(-1, 1)


def unpack(packed, odd):
    zero = jnp.zeros_like(packed)
    return jnp.concatenate([jnp.where(odd, zero, packed), jnp.where(odd, packed, zero)], axis=1)


def shards(boundary_in, row_operator, charges):
    stored, oper, charge = boundary_in[0, 0], row_operator[0, 0], charges[0, 0]
    phys_dim, bond_dim = stored.shape[0], stored.shape[2]
    half, phalf = bond_dim // 2, phys_dim // 2
    all_sites = lax.axis_size("cols")
    left_odd = (jnp.arange(bond_dim) >= charge)[None, :, None]
    low, high = stored[:, :, :half], stored[:, :, half:]
    applied = jnp.concatenate(
        [
            jnp.einsum("pq,qlc->plc", oper[:phalf], jnp.where(left_odd, high, low), preferred_element_type=jnp.float32),
            jnp.einsum("pq,qlc->plc", oper[phalf:], jnp.where(left_odd, low, high), preferred_element_type=jnp.float32),
        ]
    )
    packed = applied.astype(jnp.bfloat16).reshape(-1, half)
    packed_next = from_next(packed)
    charge_next = from_next(charges)[0, 0]
    odd = odd_rows(charge, phys_dim, bond_dim)
    flat = unpack(packed, odd)
    gram = lax.dot_general(packed, flat, (((0,), (0,)), ((), ())), preferred_element_type=jnp.float32)
    gram = sum_over_cols(gram, 0) / (all_sites * phys_dim * bond_dim / 2.0)
    grams = jnp.stack([gram[:, :half], gram[:, half:]])
    factor = jnp.linalg.cholesky(grams)
    eye = jnp.broadcast_to(jnp.eye(half, dtype=jnp.float32), factor.shape)
    inverse = lax.linalg.triangular_solve(factor, eye, left_side=True, lower=True)
    inverse_next = from_next(inverse)

    def compress(rows, inv, rows_odd):
        both = jnp.concatenate([inv[0].T, inv[1].T], axis=1)
        out = jnp.dot(rows, both, precision=HIGH, preferred_element_type=jnp.float32)
        right_odd = (jnp.arange(bond_dim) >= half)[None, :]
        return jnp.where(rows_odd == right_odd, out, 0.0).astype(jnp.bfloat16)

    compressed = compress(packed, inverse, odd)
    odd_next = odd_rows(charge_next, phys_dim, bond_dim)
    flat_next = unpack(packed_next, odd_next)
    cross = lax.dot_general(flat, flat_next, (((0,), (0,)), ((), ())), preferred_element_type=jnp.float32)
    cross = sum_over_cols(cross, 1)

    def block(inv):
        zero = jnp.zeros_like(inv[0])
        return jnp.concatenate([jnp.concatenate([inv[0], zero], 1), jnp.concatenate([zero, inv[1]], 1)], 0)

    mix_scale = 2.0 / (bond_dim * math.sqrt(all_sites * phys_dim))
    correlation = jnp.dot(block(inverse), cross, precision=HIGH)
    correlation = jnp.dot(correlation, block(inverse_next).T, precision=HIGH)
    correlation = (correlation * mix_scale).astype(jnp.bfloat16)
    compressed_next = compress(packed_next, inverse_next, odd_next)
    adjoint = jnp.dot(compressed_next, correlation.T, preferred_element_type=jnp.float32).astype(jnp.bfloat16)
    adjoint = adjoint.reshape(phys_dim, bond_dim, bond_dim)
    gradient = jnp.einsum("plc,qlc->pq", adjoint, stored, preferred_element_type=jnp.float32) / bond_dim
    return (compressed.reshape(boundary_in.shape), gradient[None, None])


def solution(mesh):
    return jax.shard_map(
        shards,
        mesh=mesh,
        in_specs=(
            P("rows", "cols", None, None, None),
            P("rows", "cols", None, None),
            P("rows", "cols"),
        ),
        out_specs=(P("rows", "cols", None, None, None), P("rows", "cols", None, None)),
        check_vma=False,
    )
```

time: 585 us -> 130 us (0.22)
  waiting for transfers between devices: 463 us -> 0.01 us
  Pallas kernels: 0 us -> 43.1 us
  between operations: 15.9 us -> 1.62 us
  local copies, waits for them, and re-layouts: 24.7 us -> 11.1 us
    psum x2 -> x0, waiting for transfers between devices: 295 us -> none  [the longest x1 159 us: from_root(): return lax.psum(jnp.where(mine, array, jnp.zeros_like(array)), axis)]
    ppermute x2 -> x3, waiting for transfers between devices: 87.9 us -> 0.01 us  [from_next(): return lax.ppermute(value, 'rows', [(r + 1, r) for r in range(count - 1)])]
    all_gather x1 -> x0, waiting for transfers between devices: 80.7 us -> none  [prefix(): gathered = lax.all_gather(part, axis)]
    pallas_call x0 -> x2, Pallas kernels: none -> 43.1 us  [sum_over_cols(): pl.pallas_call(functools.partial(sum_kernel, count), out_shape=jax.ShapeD...]
    another operation x21 -> x1, local copies, waits for them, and re-layouts: 12.4 us -> 0.09 us  [shards(): grams = jnp.stack([gram[:, :half], gram[:, half:]])]
    another operation x9 -> x8, other arithmetic: 53.7 us -> 43.4 us  [the longest x4 23.6 us: shards(): factor = jnp.linalg.cholesky(grams)]
    while x2 -> x0, local copies, waits for them, and re-layouts: 9.12 us -> none  [prefix(): return lax.fori_loop(0, place, one, state)]
    select_n x1 -> x3, other arithmetic: 0.73 us -> 7.44 us  [the longest x2 5.68 us: unpack(): jnp.where(odd, zero, packed)]
  transfers between devices with their start and end apart: 5 -> 3, of which waited for: 5 -> 0; matrix products, arithmetic and copies ran while one was open for 1% -> 51% of each run, Pallas kernels for 0% -> 18%
where the time goes in v1:
time: 130 us; the launch traced here: 128 us
  other arithmetic  52.7 us (41%)
  Pallas kernels  43.1 us (33%)
  matrix products  15.1 us (12%)
  local copies, waits for them, and re-layouts  11.1 us (9%)
  starting transfers between devices  4.06 us (3%)
  between operations  1.62 us (1%)
    pallas_call x2, Pallas kernels, sum_over_cols(): pl.pallas_call(functools.partial(sum_kernel, count), out_shape=jax.ShapeD...  43.1 us
    another operation x4, other arithmetic, shards(): factor = jnp.linalg.cholesky(grams)  23.6 us
    another operation x3, other arithmetic, shards(): lax.linalg.triangular_solve(factor, eye, left_side=True, lower=True)  19.8 us
    dot_general x2, matrix products, compress(): jnp.dot(rows, both, precision=HIGH, preferred_element_type=jnp.float32)  6.8 us
    select_n x2, other arithmetic, unpack(): jnp.where(odd, zero, packed)  5.68 us
    ppermute x3, starting transfers between devices, from_next(): return lax.ppermute(value, 'rows', [(r + 1, r) for r in range(count - 1)])  4.06 us
    dot_general x1, matrix products, shards(): jnp.einsum('plc,qlc->pq', adjoint, stored, preferred_element_type=jnp.flo...  3.78 us
    reshape x1, local copies, waits for them, and re-layouts, shards(): adjoint = adjoint.reshape(phys_dim, bond_dim, bond_dim)  3.14 us
  transfers between devices with their start and end apart: 3, of which 0 were waited for; matrix products, arithmetic and copies ran while one was open for 51% of the time, Pallas kernels for 18%

profile of v1, /device:TPU:1, one launch (start us, length us, event | category | flops | bytes accessed | tf_op | source)
XLA Modules:
  0.0 127.7 jit_solution(14249835365407246787)
XLA Ops:
  0.6 1.3 %collective-permute-start = (s32[1,1]{1,0:T(1,128)}, s32[1,1]{1,0:T(1,128)}, u32[]{:S(2)}, u32[]{:S(2)}) collective-permute-start(s32[1,1]{1,0:T(1,128)} %param.5), channel_id=1, source_target_pairs={{32,0},{64,32},{96,64},{128,96},{160,128},{192,160},{224,192},{256... | collective-permute-start | bytes 20 | tf_op jit(solution)/shard_map/ppermute | solution.py:17
  2.6 0.0 copy-start.5
  2.6 1.8 %broadcast_select_fusion.1 = (bf16[16,256,128]{2,1,0:T(8,128)(2,1)S(1)}, bf16[16,256,128]{2,1,0:T(8,128)(2,1)S(1)}) fusion(pred[256]{0:T(512)(128)(4,1)S(1)} %iota_compare_fusion.10, bf16[16,256,256]{2,1,0:T(8,128)(2,1)} %bitcast.72), kind=kLoop, calls=%fused_computation.24 | loop fusion | flops 1048576 | bytes 4194560 | tf_op jit(solution)/shard_map/jit(_where)/select_n | solution.py:129
  4.4 0.0 copy-done.5
  4.4 0.7 fusion.7
  5.0 0.7 fusion.8
  5.7 0.2 pad_maximum_fusion.3
  5.9 0.3 copy.22
  6.2 1.3 %collective-permute-start.1 = (bf16[4096,128]{1,0:T(8,128)(2,1)S(1)}, bf16[4096,128]{1,0:T(8,128)(2,1)}, u32[]{:S(2)}, u32[]{:S(2)}) collective-permute-start(bf16[4096,128]{1,0:T(8,128)(2,1)S(1)} %bitcast.74), channel_id=1, source_target_pairs={{32,0},{64,32},{96,64},{128,96},{160,128},{192,160},{224,192},{256... | collective-permute-start | bytes 3145736 | tf_op jit(solution)/shard_map/ppermute | solution.py:17
  7.6 0.0 collective-permute-done
  7.6 0.6 iota_compare_fusion.8
  8.2 0.1 broadcast_xor_fusion
  8.3 2.2 %broadcast_select_fusion.5 = (bf16[4096,128]{1,0:T(8,128)(2,1)S(1)}, bf16[4096,128]{1,0:T(8,128)(2,1)S(1)}) fusion(pred[4096]{0:T(1024)(128)(4,1)S(1)} %xor.43, bf16[16,256,128]{2,1,0:T(8,128)(2,1)S(1)} %copy.22), kind=kLoop, calls=%fused_computation.28 | loop fusion | flops 1048576 | bytes 3149824 | tf_op jit(solution)/shard_map/jit(_where)/select_n | solution.py:117
  10.5 0.0 copy-start.1
  10.5 0.0 copy-start.3
  10.5 0.9 copy-done.1
  11.4 0.4 copy-done.3
  11.8 0.5 fusion.6
  12.3 0.7 reshape.87.part_ref
  13.0 0.4 copy-done
  13.5 3.1 %copy.28 = bf16[16,256,256]{1,0,2:T(8,128)(2,1)} copy(bf16[16,256,256]{2,1,0:T(8,128)(2,1)S(1)} %bitcast.73) | data formatting | bytes 4194304 | tf_op jit(solution)/shard_map/squeeze | solution.py:121
  16.6 22.6 %sum_over_cols.2 = f32[32,8,128]{2,1,0:T(8,128)} custom-call(f32[32,8,128]{2,1,0:T(8,128)} %reshape.87.part_ref), custom_call_target="tpu_custom_call" | custom-call | flops 32768 | bytes 524288 | tf_op jit(solution)/shard_map/sum_over_cols/pallas_call | solution.py:89
  39.1 0.9 broadcast_multiply_fusion
  40.1 0.1 copy.31
  40.2 0.1 copy.30
  40.3 0.1 copy.25
  40.5 23.5 %custom-call.7 = f32[2,128,128]{2,1,0:T(8,128)S(1)} custom-call(f32[2,128,128]{2,1,0:T(8,128)S(1)} %fusion.33), custom_call_target="Cholesky" | custom-call | tf_op jit(solution)/shard_map/jit(cholesky)/cholesky | solution.py:141
  64.0 0.1 compare_reduce_fusion
  64.1 0.1 select_bitcast_fusion
  64.2 19.7 %custom-call.8 = f32[2,1,128,128]{2,3,1,0:T(8,128)S(1)} custom-call(f32[2,1,128,128]{3,2,1,0:T(8,128)S(1)} %select_bitcast_fusion), custom_call_target="InvertDiagBlocksLowerTriangular" | custom-call | tf_op jit(solution)/shard_map/triangular_solve | solution.py:143
  83.9 0.4 fusion.31
  84.3 1.5 %collective-permute-start.2 = (f32[2,128,128]{2,1,0:T(8,128)S(1)}, f32[2,128,128]{2,1,0:T(8,128)S(1)}, u32[]{:S(2)}, u32[]{:S(2)}) collective-permute-start(f32[2,128,128]{2,1,0:T(8,128)S(1)} %fusion.31), channel_id=1, source_target_pairs={{32,0},{64,32},{96,64},{128,96},{160,128},{192,160},{224,192},{256... | collective-permute-start | bytes 393224 | tf_op jit(solution)/shard_map/ppermute | solution.py:17
  85.8 3.7 %fusion = bf16[4096,256]{1,0:T(8,128)(2,1)} fusion(bf16[4096,128]{1,0:T(8,128)(2,1)S(1)} %bitcast.76, pred[256]{0:T(512)(128)(4,1)S(1)} %iota_compare_fusion.9, pred[4096]{0:T(1024)(128)(4,1)S(1)} %xor.43, f32[128,128]{0,1:T(8,128)S(1)} %get-tuple-element.14, f32[128,128]{0,1:T(8,128)S(1)} %get-tuple-element.13), kind=kOutput, calls=%fused_computation.2 | convolution fusion | flops 1613791232 | bytes 3281152 | tf_op jit(solution)/shard_map/dot_general | solution.py:148
  89.5 0.0 collective-permute-done.1
  89.5 3.5 %broadcast_select_fusion.3 = (bf16[4096,128]{1,0:T(8,128)(2,1)S(1)}, bf16[4096,128]{1,0:T(8,128)(2,1)S(1)}) fusion(bf16[4096,128]{1,0:T(8,128)(2,1)} %collective-permute-done.1, pred[4096]{0:T(1024)(128)(4,1)S(1)} %xor.46), kind=kLoop, calls=%fused_computation.26 | loop fusion | flops 1048576 | bytes 3149824 | tf_op jit(solution)/shard_map/jit(_where)/select_n | solution.py:117
  93.1 0.0 copy-done.2
  93.1 0.0 copy-done.4
  93.1 0.7 fusion.2
  93.8 0.7 reshape.89.part_ref
  94.5 0.0 collective-permute-done.2
  94.6 20.6 %sum_over_cols.3 = f32[32,16,128]{2,1,0:T(8,128)} custom-call(f32[32,16,128]{2,1,0:T(8,128)} %reshape.89.part_ref), custom_call_target="tpu_custom_call" | custom-call | flops 65536 | bytes 1048576 | tf_op jit(solution)/shard_map/sum_over_cols/pallas_call | solution.py:89
  115.2 1.0 reshape.90
  116.2 0.4 fusion.17
  116.6 0.4 fusion.9
  117.0 3.1 %fusion.1 = bf16[4096,256]{1,0:T(8,128)(2,1)S(1)} fusion(bf16[4096,128]{1,0:T(8,128)(2,1)} %collective-permute-done.1, pred[256]{0:T(512)(128)(4,1)S(1)} %iota_compare_fusion.9, pred[4096]{0:T(1024)(128)(4,1)S(1)} %xor.46, f32[128,128]{0,1:T(8,128)S(1)} %get-tuple-element.10, f32[128,128]{0,1:T(8,128)S(1)} %get-tuple-element.9), kind=kOutput, calls=%fused_computation.3 | convolution fusion | flops 1613791232 | bytes 3281152 | tf_op jit(solution)/shard_map/dot_general | solution.py:148
  120.1 0.7 convolution_convert_fusion
  120.8 3.1 %copy.27 = bf16[16,256,256]{1,0,2:T(8,128)(2,1)} copy(bf16[16,256,256]{2,1,0:T(8,128)(2,1)S(1)} %bitcast.71) | data formatting | bytes 4194304 | tf_op jit(solution)/shard_map/reshape | solution.py:168
  123.9 3.8 %fusion.11 = f32[1,1,16,16]{3,2,1,0:T(8,128)} fusion(bf16[16,256,256]{1,0,2:T(8,128)(2,1)} %copy.27, bf16[16,256,256]{1,0,2:T(8,128)(2,1)} %copy.28), kind=kOutput, calls=%fused_computation.19 | convolution fusion | flops 33554688 | bytes 4195328 | tf_op jit(solution)/shard_map/plc,qlc->pq/dot_general | solution.py:169
  (18 shorter events, 0.2 us)
Async XLA Ops:
  0.6 6.9 %collective-permute-start = (s32[1,1]{1,0:T(1,128)}, s32[1,1]{1,0:T(1,128)}, u32[]{:S(2)}, u32[]{:S(2)}) collective-permute-start(s32[1,1]{1,0:T(1,128)} %param.5), channel_id=1, source_target_pairs={{32,0},{64,32},{96,64},{128,96},{160,128},{192,160},{224,192},{256... | collective-permute-start | bytes 20 | tf_op jit(solution)/shard_map/ppermute | solution.py:17
  2.6 1.8 %copy-start.5 = (bf16[1,1,16,16]{3,2,1,0:T(8,128)(2,1)S(1)}, bf16[1,1,16,16]{3,2,1,0:T(8,128)(2,1)}, u32[]{:S(2)}) copy-start(bf16[1,1,16,16]{3,2,1,0:T(8,128)(2,1)} %param.4) | copy-start | bytes 1540
  6.2 83.3 %collective-permute-start.1 = (bf16[4096,128]{1,0:T(8,128)(2,1)S(1)}, bf16[4096,128]{1,0:T(8,128)(2,1)}, u32[]{:S(2)}, u32[]{:S(2)}) collective-permute-start(bf16[4096,128]{1,0:T(8,128)(2,1)S(1)} %bitcast.74), channel_id=1, source_target_pairs={{32,0},{64,32},{96,64},{128,96},{160,128},{192,160},{224,192},{256... | collective-permute-start | bytes 3145736 | tf_op jit(solution)/shard_map/ppermute | solution.py:17
  10.5 1.0 copy-start.1
  10.5 1.3 %copy-start.3 = (bf16[4096,128]{1,0:T(8,128)(2,1)}, bf16[4096,128]{1,0:T(8,128)(2,1)S(1)}, u32[]{:S(2)}) copy-start(bf16[4096,128]{1,0:T(8,128)(2,1)S(1)} %get-tuple-element.7) | copy-start | bytes 3145732
  11.8 1.6 %copy-start = (bf16[1,1,16,256,256]{4,3,2,1,0:T(8,128)(2,1)S(1)}, bf16[1,1,16,256,256]{4,3,2,1,0:T(8,128)(2,1)}, u32[]{:S(2)}) copy-start(bf16[1,1,16,256,256]{4,3,2,1,0:T(8,128)(2,1)} %param.3) | copy-start | bytes 6291460
  84.3 10.3 %collective-permute-start.2 = (f32[2,128,128]{2,1,0:T(8,128)S(1)}, f32[2,128,128]{2,1,0:T(8,128)S(1)}, u32[]{:S(2)}, u32[]{:S(2)}) collective-permute-start(f32[2,128,128]{2,1,0:T(8,128)S(1)} %fusion.31), channel_id=1, source_target_pairs={{32,0},{64,32},{96,64},{128,96},{160,128},{192,160},{224,192},{256... | collective-permute-start | bytes 393224 | tf_op jit(solution)/shard_map/ppermute | solution.py:17
  89.5 3.5 %copy-start.2 = (bf16[4096,128]{1,0:T(8,128)(2,1)S(1)}, bf16[4096,128]{1,0:T(8,128)(2,1)}, u32[]{:S(2)}) copy-start(bf16[4096,128]{1,0:T(8,128)(2,1)} %copy-done.1) | copy-start | bytes 3145732
  89.5 3.6 %copy-start.4 = (bf16[4096,128]{1,0:T(8,128)(2,1)S(1)}, bf16[4096,128]{1,0:T(8,128)(2,1)}, u32[]{:S(2)}) copy-start(bf16[4096,128]{1,0:T(8,128)(2,1)} %copy-done.3) | copy-start | bytes 3145732

commit v2 on v1

--- a/solution.py
+++ b/solution.py
@@ -104,6 +104,167 @@
         name="sum_over_cols",
     )(part.reshape(pieces))
     return total.reshape(shape)
+
+
+def split3(x):
+    high = x.astype(jnp.bfloat16).astype(jnp.float32)
+    rest = x - high
+    mid = rest.astype(jnp.bfloat16).astype(jnp.float32)
+    return high, mid, rest - mid
+
+
+def invert_factor(state, size):
+    step = 8
+    blocks = range(state.shape[0])
+    lane = lax.broadcasted_iota(jnp.int32, (step, size), 1)
+    sub = lax.broadcasted_iota(jnp.int32, (step, size), 0)
+    lane_all = lax.broadcasted_iota(jnp.int32, (size, size), 1)
+    for base in range(0, size, step):
+        stop = base + step
+        own = (lane >= base) & (lane < stop)
+        for b in blocks:
+            rows = state[b, base:stop, :]
+            columns = [jnp.broadcast_to(rows[:, base + k : base + k + 1], (step, size)) for k in range(step)]
+            unit = jnp.where(lane == sub + base, 1.0, 0.0)
+            pivots = jnp.ones((step, size), jnp.float32)
+            for k in range(step):
+                pivot = jnp.broadcast_to(columns[k][k : k + 1, :], (step, size))
+                pivots = jnp.where(sub == k, pivot, pivots)
+                factor = jnp.where(sub > k, columns[k] / pivot, 0.0)
+                for later in range(k + 1, step):
+                    columns[later] = columns[later] - factor * jnp.broadcast_to(columns[later][k : k + 1, :], (step, size))
+                rows = rows - factor * jnp.broadcast_to(rows[k : k + 1, :], (step, size))
+                unit = unit - factor * jnp.broadcast_to(unit[k : k + 1, :], (step, size))
+            done = jnp.where(own, unit, rows)
+            if stop < size:
+                lh, lm, ll = split3(rows / pivots)
+                rh, rm, rl = split3(done)
+                left = jnp.concatenate([lh, lh, lm, lh, ll, lm], axis=0).astype(jnp.bfloat16)
+                right = jnp.concatenate([rh, rm, rh, rl, rh, rm], axis=0).astype(jnp.bfloat16)
+                update = lax.dot_general(left, right, (((0,), (0,)), ((), ())), preferred_element_type=jnp.float32)
+                below = state[b, stop:, :]
+                inside = (lane_all[stop:] >= base) & (lane_all[stop:] < stop)
+                state[b, stop:, :] = jnp.where(inside, 0.0, below) - update[stop:]
+            state[b, base:stop, :] = jnp.where(lane <= sub + base, done * lax.rsqrt(pivots), 0.0)
+
+
+def middle_kernel(count, sections, scale, gram_ref, part_ref, inverse_ref, next_ref, total_ref, state, arrived, landed, whole, send_a, recv_a, send_b, recv_b, send_c, recv_c):
+    me = lax.axis_index("cols")
+    row = lax.axis_index("rows")
+    size = state.shape[1]
+    below = lax.rem(row + sections - 1, sections)
+    above = lax.rem(row + 1, sections)
+
+    def after(k):
+        return lax.rem(me + k, count)
+
+    def before(k):
+        return lax.rem(me + count - k, count)
+
+    barrier = pltpu.get_barrier_semaphore()
+    pl.semaphore_signal(barrier, inc=1, device_id={"rows": below}, device_id_type=MESH)
+    pl.semaphore_signal(barrier, inc=1, device_id={"rows": above}, device_id_type=MESH)
+
+    @pl.loop(1, count)
+    def _(k):
+        pl.semaphore_signal(barrier, inc=1, device_id={"cols": after(k)}, device_id_type=MESH)
+
+    pl.semaphore_wait(barrier, count + 1)
+
+    def scatter(k):
+        return pltpu.make_async_remote_copy(
+            src_ref=part_ref.at[after(k)],
+            dst_ref=landed.at[k],
+            send_sem=send_a.at[k],
+            recv_sem=recv_a.at[k],
+            device_id={"cols": after(k)},
+            device_id_type=MESH,
+        )
+
+    @pl.loop(1, count)
+    def _(k):
+        scatter(k).start()
+
+    landed[0] = part_ref[me]
+    state[0] = gram_ref[:, :size] * scale
+    state[1] = gram_ref[:, size:] * scale
+    invert_factor(state, size)
+    down = pltpu.make_async_remote_copy(
+        src_ref=state,
+        dst_ref=arrived,
+        send_sem=send_c,
+        recv_sem=recv_c,
+        device_id={"rows": below},
+        device_id_type=MESH,
+    )
+    down.start()
+
+    @pl.loop(1, count)
+    def _(k):
+        scatter(k).wait_recv()
+
+    whole[me] = jnp.sum(landed[...], axis=0)
+
+    def gather(k, owner):
+        return pltpu.make_async_remote_copy(
+            src_ref=whole.at[owner],
+            dst_ref=whole.at[owner],
+            send_sem=send_b.at[k],
+            recv_sem=recv_b.at[k],
+            device_id={"cols": after(k)},
+            device_id_type=MESH,
+        )
+
+    @pl.loop(1, count)
+    def _(k):
+        gather(k, me).start()
+
+    inverse_ref[...] = state[...]
+
+    @pl.loop(1, count)
+    def _(k):
+        gather(k, before(k)).wait_recv()
+
+    total_ref[...] = whole[...]
+    down.wait_recv()
+    next_ref[...] = arrived[...]
+    down.wait_send()
+
+    @pl.loop(1, count)
+    def _(k):
+        scatter(k).wait_send()
+        gather(k, me).wait_send()
+
+
+def invert_and_sum(gram, scale, part, collective_id):
+    count, sections = lax.axis_size("cols"), lax.axis_size("rows")
+    size = gram.shape[0]
+    blocks = jax.ShapeDtypeStruct((2, size, size), jnp.float32)
+    pieces = jax.ShapeDtypeStruct((count, part.size // count // 128, 128), jnp.float32)
+    vmem = pl.BlockSpec(memory_space=pltpu.VMEM)
+    inverse, following, total = pl.pallas_call(
+        functools.partial(middle_kernel, count, sections, scale),
+        out_shape=(blocks, blocks, pieces),
+        in_specs=[vmem, vmem],
+        out_specs=(vmem, vmem, vmem),
+        scratch_shapes=[
+            pltpu.VMEM(blocks.shape, jnp.float32),
+            pltpu.VMEM(blocks.shape, jnp.float32),
+            pltpu.VMEM(pieces.shape, jnp.float32),
+            pltpu.VMEM(pieces.shape, jnp.float32),
+            pltpu.SemaphoreType.DMA((count,)),
+            pltpu.SemaphoreType.DMA((count,)),
+            pltpu.SemaphoreType.DMA((count,)),
+            pltpu.SemaphoreType.DMA((count,)),
+            pltpu.SemaphoreType.DMA,
+            pltpu.SemaphoreType.DMA,
+        ],
+        compiler_params=pltpu.CompilerParams(collective_id=collective_id, has_side_effects=True),
+        cost_estimate=pl.CostEstimate(flops=part.size, bytes_accessed=16 * part.size, transcendentals=0),
+        name="invert_and_sum",
+    )(gram, part.reshape(pieces.shape))
+    is_last = lax.axis_index("rows") == sections - 1
+    return inverse, jnp.where(is_last, 0.0, following), total.reshape(part.shape)
 
 
 def odd_rows(charge, phys_dim, bond_dim):
@@ -136,12 +297,12 @@
     odd = odd_rows(charge, phys_dim, bond_dim)
     flat = unpack(packed, odd)
     gram = lax.dot_general(packed, flat, (((0,), (0,)), ((), ())), preferred_element_type=jnp.float32)
-    gram = sum_over_cols(gram, 0) / (all_sites * phys_dim * bond_dim / 2.0)
-    grams = jnp.stack([gram[:, :half], gram[:, half:]])
-    factor = jnp.linalg.cholesky(grams)
-    eye = jnp.broadcast_to(jnp.eye(half, dtype=jnp.float32), factor.shape)
-    inverse = lax.linalg.triangular_solve(factor, eye, left_side=True, lower=True)
-    inverse_next = from_next(inverse)
+    gram = sum_over_cols(gram, 0)
+    odd_next = odd_rows(charge_next, phys_dim, bond_dim)
+    flat_next = unpack(packed_next, odd_next)
+    cross = lax.dot_general(flat, flat_next, (((0,), (0,)), ((), ())), preferred_element_type=jnp.float32)
+    scale = 2.0 / (all_sites * phys_dim * bond_dim)
+    inverse, inverse_next, cross = invert_and_sum(gram, scale, cross, 1)
 
     def compress(rows, inv, rows_odd):
         both = jnp.concatenate([inv[0].T, inv[1].T], axis=1)
@@ -150,10 +311,6 @@
         return jnp.where(rows_odd == right_odd, out, 0.0).astype(jnp.bfloat16)
 
     compressed = compress(packed, inverse, odd)
-    odd_next = odd_rows(charge_next, phys_dim, bond_dim)
-    flat_next = unpack(packed_next, odd_next)
-    cross = lax.dot_general(flat, flat_next, (((0,), (0,)), ((), ())), preferred_element_type=jnp.float32)
-    cross = sum_over_cols(cross, 1)
 
     def block(inv):
         zero = jnp.zeros_like(inv[0])

time: 130 us -> 90.9 us (0.70); the launches traced: 128 us -> 90.4 us
  other arithmetic: 52.7 us -> 9.05 us
  Pallas kernels: 43.1 us -> 51.1 us
  starting transfers between devices: 4.06 us -> 2.72 us
    another operation x8 -> x0, other arithmetic: 43.4 us -> none  [the longest x4 23.6 us: shards(): factor = jnp.linalg.cholesky(grams)]
    pallas_call x0 -> x1, Pallas kernels: none -> 28.5 us  [invert_and_sum(): pl.pallas_call(functools.partial(middle_kernel, count, sections, scale),...]
    pallas_call x2 -> x1, Pallas kernels: 43.1 us -> 22.6 us  [sum_over_cols(): pl.pallas_call(functools.partial(sum_kernel, count), out_shape=jax.ShapeD...]
    unnamed x14 -> x4, local copies, waits for them, and re-layouts: 1.96 us -> 0.01 us
    reshape x0 -> x2, local copies, waits for them, and re-layouts: none -> 1.75 us  [the longest x1 1.03 us: invert_and_sum(): total.reshape(part.shape)]
    ppermute x3 -> x2, starting transfers between devices: 4.06 us -> 2.72 us  [from_next(): return lax.ppermute(value, 'rows', [(r + 1, r) for r in range(count - 1)])]
  transfers between devices with their start and end apart: 3 -> 2, of which waited for: 0 -> 0; matrix products, arithmetic and copies ran while one was open for 51% -> 14% of each run, Pallas kernels for 18% -> 25%
where the time goes in v2:
time: 90.9 us; the launch traced here: 90.4 us
  Pallas kernels  51.1 us (56%)
  matrix products  14.7 us (16%)
  local copies, waits for them, and re-layouts  11.4 us (13%)
  other arithmetic  9.05 us (10%)
  starting transfers between devices  2.72 us (3%)
  between operations  1.49 us (2%)
    pallas_call x1, Pallas kernels, invert_and_sum(): pl.pallas_call(functools.partial(middle_kernel, count, sections, scale),...  28.5 us
    pallas_call x1, Pallas kernels, sum_over_cols(): pl.pallas_call(functools.partial(sum_kernel, count), out_shape=jax.ShapeD...  22.6 us
    dot_general x2, matrix products, compress(): jnp.dot(rows, both, precision=HIGH, preferred_element_type=jnp.float32)  6.77 us
    select_n x2, other arithmetic, unpack(): jnp.where(odd, zero, packed)  5.53 us
    dot_general x1, matrix products, shards(): jnp.einsum('plc,qlc->pq', adjoint, stored, preferred_element_type=jnp.flo...  3.78 us
    squeeze x1, local copies, waits for them, and re-layouts, shards(): boundary_in[0, 0]  3.12 us
    reshape x1, local copies, waits for them, and re-layouts, shards(): adjoint = adjoint.reshape(phys_dim, bond_dim, bond_dim)  3.07 us
    ppermute x2, starting transfers between devices, from_next(): return lax.ppermute(value, 'rows', [(r + 1, r) for r in range(count - 1)])  2.72 us
  transfers between devices with their start and end apart: 2, of which 0 were waited for; matrix products, arithmetic and copies ran while one was open for 14% of the time, Pallas kernels for 25%

profile of v2, /device:TPU:1, one launch (start us, length us, event | category | flops | bytes accessed | tf_op | source)
XLA Modules:
  0.0 90.4 jit_solution(11997702127469749709)
XLA Ops:
  0.6 1.3 %collective-permute-start = (s32[1,1]{1,0:T(1,128)}, s32[1,1]{1,0:T(1,128)}, u32[]{:S(2)}, u32[]{:S(2)}) collective-permute-start(s32[1,1]{1,0:T(1,128)} %param.5), channel_id=1, source_target_pairs={{32,0},{64,32},{96,64},{128,96},{160,128},{192,160},{224,192},{256... | collective-permute-start | bytes 20 | tf_op jit(solution)/shard_map/ppermute | solution.py:17
  2.6 0.0 copy-start.1
  2.6 1.8 %broadcast_select_fusion.1 = (bf16[16,256,128]{2,1,0:T(8,128)(2,1)S(1)}, bf16[16,256,128]{2,1,0:T(8,128)(2,1)S(1)}) fusion(pred[256]{0:T(512)(128)(4,1)S(1)} %iota_compare_fusion.8, bf16[16,256,256]{2,1,0:T(8,128)(2,1)} %bitcast.61), kind=kLoop, calls=%fused_computation.24 | loop fusion | flops 1048576 | bytes 4194560 | tf_op jit(solution)/shard_map/jit(_where)/select_n | solution.py:290
  4.4 0.0 copy-done.1
  4.4 0.7 fusion.7
  5.0 0.7 fusion.8
  5.7 0.0 copy-start
  5.7 0.2 pad_maximum_fusion.3
  5.9 0.3 copy.11
  6.2 1.4 %collective-permute-start.1 = (bf16[4096,128]{1,0:T(8,128)(2,1)S(1)}, bf16[4096,128]{1,0:T(8,128)(2,1)}, u32[]{:S(2)}, u32[]{:S(2)}) collective-permute-start(bf16[4096,128]{1,0:T(8,128)(2,1)S(1)} %bitcast.63), channel_id=1, source_target_pairs={{32,0},{64,32},{96,64},{128,96},{160,128},{192,160},{224,192},{256... | collective-permute-start | bytes 3145736 | tf_op jit(solution)/shard_map/ppermute | solution.py:17
  7.7 0.0 copy-done
  7.7 3.1 %copy.13 = bf16[16,256,256]{1,0,2:T(8,128)(2,1)} copy(bf16[16,256,256]{2,1,0:T(8,128)(2,1)S(1)} %bitcast.62) | data formatting | bytes 4194304 | tf_op jit(solution)/shard_map/squeeze | solution.py:282
  10.8 0.0 collective-permute-done
  10.8 0.6 iota_compare_fusion.6
  11.4 0.1 broadcast_xor_fusion
  11.5 2.2 %broadcast_select_fusion.5 = (bf16[4096,128]{1,0:T(8,128)(2,1)S(1)}, bf16[4096,128]{1,0:T(8,128)(2,1)S(1)}) fusion(pred[4096]{0:T(1024)(128)(4,1)S(1)} %xor.43, bf16[16,256,128]{2,1,0:T(8,128)(2,1)S(1)} %copy.11), kind=kLoop, calls=%fused_computation.28 | loop fusion | flops 1048576 | bytes 3149824 | tf_op jit(solution)/shard_map/jit(_where)/select_n | solution.py:278
  13.6 0.5 fusion.6
  14.1 0.7 reshape.77.part_ref
  14.8 22.6 %sum_over_cols.1 = f32[32,8,128]{2,1,0:T(8,128)} custom-call(f32[32,8,128]{2,1,0:T(8,128)} %reshape.77.part_ref), custom_call_target="tpu_custom_call" | custom-call | flops 32768 | bytes 524288 | tf_op jit(solution)/shard_map/sum_over_cols/pallas_call | solution.py:89
  37.4 1.6 %reshape.78.gram_ref = f32[128,256]{1,0:T(8,128)} reshape(f32[32,8,128]{2,1,0:T(8,128)} %sum_over_cols.1) | data formatting | bytes 262144 | tf_op jit(solution)/shard_map/reshape | solution.py:106
  39.0 0.0 collective-permute-done.1
  39.0 3.4 %broadcast_select_fusion.3 = (bf16[4096,128]{1,0:T(8,128)(2,1)S(1)}, bf16[4096,128]{1,0:T(8,128)(2,1)S(1)}) fusion(bf16[4096,128]{1,0:T(8,128)(2,1)} %collective-permute-done.1, pred[4096]{0:T(1024)(128)(4,1)S(1)} %xor.46), kind=kLoop, calls=%fused_computation.26 | loop fusion | flops 1048576 | bytes 3149824 | tf_op jit(solution)/shard_map/jit(_where)/select_n | solution.py:278
  42.4 0.8 fusion.2
  43.1 0.7 reshape.79.part_ref
  43.9 28.5 %invert_and_sum.1 = (f32[2,128,128]{2,1,0:T(8,128)}, f32[2,128,128]{2,1,0:T(8,128)}, f32[32,16,128]{2,1,0:T(8,128)}) custom-call(f32[128,256]{1,0:T(8,128)} %reshape.78.gram_ref, f32[32,16,128]{2,1,0:T(8,128)} %reshape.79.part_ref), custom_call_target="tpu_custom_call" | custom-call | flops 65536 | bytes 1048576 | tf_op jit(solution)/shard_map/invert_and_sum/pallas_call | solution.py:245
  72.4 0.9 slice_bitcast_fusion.7
  73.3 1.0 %reshape.81 = f32[256,256]{1,0:T(8,128)S(1)} reshape(f32[32,16,128]{2,1,0:T(8,128)} %get-tuple-element.7) | data formatting | bytes 524288 | tf_op jit(solution)/shard_map/reshape | solution.py:267
  74.3 0.9 %broadcast_select_fusion.6 = f32[2,128,128]{2,1,0:T(8,128)S(1)} fusion(f32[2,128,128]{2,1,0:T(8,128)} %get-tuple-element.6, pred[]{:T(512)S(6)} %eq.34), kind=kLoop, calls=%fused_computation.50 | loop fusion | flops 32768 | bytes 262145 | tf_op jit(solution)/shard_map/jit(_where)/select_n | solution.py:267
  75.2 0.4 fusion.17
  75.6 0.4 fusion.9
  76.1 3.1 %fusion.1 = bf16[4096,256]{1,0:T(8,128)(2,1)S(1)} fusion(bf16[4096,128]{1,0:T(8,128)(2,1)} %collective-permute-done.1, pred[256]{0:T(512)(128)(4,1)S(1)} %iota_compare_fusion.7, pred[4096]{0:T(1024)(128)(4,1)S(1)} %xor.46, f32[128,128]{0,1:T(8,128)S(1)} %get-tuple-element.16, f32[128,128]{0,1:T(8,128)S(1)} %get-tuple-element.15), kind=kOutput, calls=%fused_computation.3 | convolution fusion | flops 1613791232 | bytes 3281152 | tf_op jit(solution)/shard_map/dot_general | solution.py:309
  79.1 0.7 convolution_convert_fusion
  79.9 3.1 %copy.12 = bf16[16,256,256]{1,0,2:T(8,128)(2,1)} copy(bf16[16,256,256]{2,1,0:T(8,128)(2,1)S(1)} %bitcast.60) | data formatting | bytes 4194304 | tf_op jit(solution)/shard_map/reshape | solution.py:325
  82.9 3.8 %fusion.11 = f32[1,1,16,16]{3,2,1,0:T(8,128)} fusion(bf16[16,256,256]{1,0,2:T(8,128)(2,1)} %copy.12, bf16[16,256,256]{1,0,2:T(8,128)(2,1)} %copy.13), kind=kOutput, calls=%fused_computation.19 | convolution fusion | flops 33554688 | bytes 4195328 | tf_op jit(solution)/shard_map/plc,qlc->pq/dot_general | solution.py:326
  86.7 3.7 %fusion = bf16[4096,256]{1,0:T(8,128)(2,1)} fusion(bf16[4096,128]{1,0:T(8,128)(2,1)S(1)} %bitcast.65, pred[256]{0:T(512)(128)(4,1)S(1)} %iota_compare_fusion.7, pred[4096]{0:T(1024)(128)(4,1)S(1)} %xor.43, f32[128,128]{0,1:T(8,128)S(1)} %get-tuple-element.20, f32[128,128]{0,1:T(8,128)S(1)} %get-tuple-element.19), kind=kOutput, calls=%fused_computation.2 | convolution fusion | flops 1613791232 | bytes 3281152 | tf_op jit(solution)/shard_map/dot_general | solution.py:309
  (6 shorter events, 0.1 us)
Async XLA Ops:
  0.6 10.2 %collective-permute-start = (s32[1,1]{1,0:T(1,128)}, s32[1,1]{1,0:T(1,128)}, u32[]{:S(2)}, u32[]{:S(2)}) collective-permute-start(s32[1,1]{1,0:T(1,128)} %param.5), channel_id=1, source_target_pairs={{32,0},{64,32},{96,64},{128,96},{160,128},{192,160},{224,192},{256... | collective-permute-start | bytes 20 | tf_op jit(solution)/shard_map/ppermute | solution.py:17
  2.6 1.8 %copy-start.1 = (bf16[1,1,16,16]{3,2,1,0:T(8,128)(2,1)S(1)}, bf16[1,1,16,16]{3,2,1,0:T(8,128)(2,1)}, u32[]{:S(2)}) copy-start(bf16[1,1,16,16]{3,2,1,0:T(8,128)(2,1)} %param.4) | copy-start | bytes 1540
  5.7 1.9 %copy-start = (bf16[1,1,16,256,256]{4,3,2,1,0:T(8,128)(2,1)S(1)}, bf16[1,1,16,256,256]{4,3,2,1,0:T(8,128)(2,1)}, u32[]{:S(2)}) copy-start(bf16[1,1,16,256,256]{4,3,2,1,0:T(8,128)(2,1)} %param.3) | copy-start | bytes 6291460
  6.2 32.8 %collective-permute-start.1 = (bf16[4096,128]{1,0:T(8,128)(2,1)S(1)}, bf16[4096,128]{1,0:T(8,128)(2,1)}, u32[]{:S(2)}, u32[]{:S(2)}) collective-permute-start(bf16[4096,128]{1,0:T(8,128)(2,1)S(1)} %bitcast.63), channel_id=1, source_target_pairs={{32,0},{64,32},{96,64},{128,96},{160,128},{192,160},{224,192},{256... | collective-permute-start | bytes 3145736 | tf_op jit(solution)/shard_map/ppermute | solution.py:17

commit v3 on v1

v3 whole, which is shorter than its diff:
```python
import functools
import math

import jax
import jax.numpy as jnp
from jax import lax
from jax.experimental import pallas as pl
from jax.experimental.pallas import tpu as pltpu
from jax.sharding import PartitionSpec as P

HIGH = lax.Precision.HIGHEST
MESH = pl.DeviceIdType.MESH


def split3(x):
    high = x.astype(jnp.bfloat16).astype(jnp.float32)
    rest = x - high
    mid = rest.astype(jnp.bfloat16).astype(jnp.float32)
    return high, mid, rest - mid


def invert_factor(state, size, first, last):
    step = 8
    blocks = range(state.shape[0])
    lane = lax.broadcasted_iota(jnp.int32, (step, size), 1)
    sub = lax.broadcasted_iota(jnp.int32, (step, size), 0)
    lane_all = lax.broadcasted_iota(jnp.int32, (size, size), 1)
    for base in range(first, last, step):
        stop = base + step
        own = (lane >= base) & (lane < stop)
        for b in blocks:
            rows = state[b, base:stop, :]
            columns = [jnp.broadcast_to(rows[:, base + k : base + k + 1], (step, size)) for k in range(step)]
            unit = jnp.where(lane == sub + base, 1.0, 0.0)
            pivots = jnp.ones((step, size), jnp.float32)
            for k in range(step):
                pivot = jnp.broadcast_to(columns[k][k : k + 1, :], (step, size))
                pivots = jnp.where(sub == k, pivot, pivots)
                factor = jnp.where(sub > k, columns[k] / pivot, 0.0)
                for later in range(k + 1, step):
                    columns[later] = columns[later] - factor * jnp.broadcast_to(columns[later][k : k + 1, :], (step, size))
                rows = rows - factor * jnp.broadcast_to(rows[k : k + 1, :], (step, size))
                unit = unit - factor * jnp.broadcast_to(unit[k : k + 1, :], (step, size))
            done = jnp.where(own, unit, rows)
            if stop < size:
                lh, lm, ll = split3(rows / pivots)
                rh, rm, rl = split3(done)
                left = jnp.concatenate([lh, lh, lm, lh, ll, lm], axis=0).astype(jnp.bfloat16)
                right = jnp.concatenate([rh, rm, rh, rl, rh, rm], axis=0).astype(jnp.bfloat16)
                update = lax.dot_general(left, right, (((0,), (0,)), ((), ())), preferred_element_type=jnp.float32)
                below = state[b, stop:, :]
                inside = (lane_all[stop:] >= base) & (lane_all[stop:] < stop)
                state[b, stop:, :] = jnp.where(inside, 0.0, below) - update[stop:]
            state[b, base:stop, :] = jnp.where(lane <= sub + base, done * lax.rsqrt(pivots), 0.0)


def exact_dot(rows, weights):
    high, mid, low = split3(weights)
    pair = jnp.concatenate([high, mid], axis=0).astype(jnp.bfloat16)
    twice = jnp.concatenate([rows, rows], axis=1)
    out = jnp.dot(twice, pair, preferred_element_type=jnp.float32)
    return out + jnp.dot(rows, low.astype(jnp.bfloat16), preferred_element_type=jnp.float32)


def unpack(rows, odd):
    wide = rows.astype(jnp.float32)
    return jnp.concatenate([jnp.where(odd, 0.0, wide), jnp.where(odd, wide, 0.0)], axis=1).astype(jnp.bfloat16)


def mask_halves(out, odd):
    half = out.shape[1] // 2
    return jnp.concatenate([jnp.where(odd, 0.0, out[:, :half]), jnp.where(odd, out[:, half:], 0.0)], axis=1).astype(jnp.bfloat16)


def whole_kernel(
    count, sections, phys, bond, scale, mix_scale,
    packed_ref, stored_hbm, charge_ref,
    out_ref, grad_ref,
    stored, ordered, packed_next, compressed_next, charge_own, charge_next,
    state, inverse_next, gram_part, gram_land, gram_all, cross_part, cross_land, cross_all,
    send_a, recv_a, send_b, recv_b, send_c, recv_c, send_d, recv_d, send_r, recv_r, load_sem,
):
    me = lax.axis_index("cols")
    row = lax.axis_index("rows")
    half = bond // 2
    below = lax.rem(row + sections - 1, sections)
    above = lax.rem(row + 1, sections)

    def after(k):
        return lax.rem(me + k, count)

    def before(k):
        return lax.rem(me + count - k, count)

    barrier = pltpu.get_barrier_semaphore()
    pl.semaphore_signal(barrier, inc=1, device_id={"rows": below}, device_id_type=MESH)
    pl.semaphore_signal(barrier, inc=1, device_id={"rows": above}, device_id_type=MESH)

    @pl.loop(1, count)
    def _(k):
        pl.semaphore_signal(barrier, inc=1, device_id={"cols": after(k)}, device_id_type=MESH)

    load = pltpu.make_async_copy(stored_hbm, stored, load_sem)
    load.start()
    charge = charge_ref[0, 0]
    charge_own[...] = jnp.full(charge_own.shape, charge, jnp.int32)
    tile = 2 * bond
    tiles = phys // 2
    place = lax.broadcasted_iota(jnp.int32, (tile, half), 0)

    def odd_rows(step, charge):
        left_odd = lax.rem(place, bond) >= charge
        phys_odd = (2 * step + place // bond) >= phys // 2
        return left_odd != phys_odd

    def rows_of(step):
        return pl.ds(pl.multiple_of(step * tile, tile), tile)

    def gram_step(step, total):
        rows = packed_ref[rows_of(step), :]
        flat = unpack(rows, odd_rows(step, charge))
        return total + lax.dot_general(rows, flat, (((0,), (0,)), ((), ())), preferred_element_type=jnp.float32)

    gram = lax.fori_loop(0, tiles, gram_step, jnp.zeros((half, bond), jnp.float32))
    gram_part[: count // 2] = gram[:, :half].reshape(count // 2, -1, half)
    gram_part[count // 2 :] = gram[:, half:].reshape(count // 2, -1, half)
    pl.semaphore_wait(barrier, count + 1)

    def to_below(source, target, index):
        return pltpu.make_async_remote_copy(
            src_ref=source, dst_ref=target, send_sem=send_r.at[index], recv_sem=recv_r.at[index],
            device_id={"rows": below}, device_id_type=MESH,
        )

    def scatter(k, part, land, send, recv):
        return pltpu.make_async_remote_copy(
            src_ref=part.at[after(k)], dst_ref=land.at[k], send_sem=send.at[k], recv_sem=recv.at[k],
            device_id={"cols": after(k)}, device_id_type=MESH,
        )

    def gather(k, owner, whole, send, recv):
        return pltpu.make_async_remote_copy(
            src_ref=whole.at[owner], dst_ref=whole.at[owner], send_sem=send.at[k], recv_sem=recv.at[k],
            device_id={"cols": after(k)}, device_id_type=MESH,
        )

    @pl.loop(1, count)
    def _(k):
        scatter(k, gram_part, gram_land, send_a, recv_a).start()

    rows_down = to_below(packed_ref, packed_next, 0)
    rows_down.start()
    charge_down = to_below(charge_own, charge_next, 1)
    charge_down.start()
    gram_land[0] = gram_part[me]
    load.wait()
    group = bond // phys
    block = group * phys

    def reorder(step, source, target):
        left = pl.ds(pl.multiple_of(step * group, group), group)
        rows = source[:, left, :].astype(jnp.float32)
        rows = jnp.swapaxes(rows, 0, 1).reshape(block, rows.shape[2])
        target[pl.ds(pl.multiple_of(step * block, block), block), :] = rows.astype(jnp.bfloat16)

    @pl.loop(0, bond // group // 2)
    def _(step):
        reorder(step, stored, ordered)

    @pl.loop(1, count)
    def _(k):
        scatter(k, gram_part, gram_land, send_a, recv_a).wait_recv()

    gram_all[me] = jnp.sum(gram_land[...], axis=0)

    @pl.loop(1, count)
    def _(k):
        gather(k, me, gram_all, send_b, recv_b).start()

    @pl.loop(bond // group // 2, bond // group)
    def _(step):
        reorder(step, stored, ordered)

    @pl.loop(1, count)
    def _(k):
        gather(k, before(k), gram_all, send_b, recv_b).wait_recv()

    state[0] = gram_all[: count // 2].reshape(half, half) * scale
    state[1] = gram_all[count // 2 :].reshape(half, half) * scale
    invert_factor(state, half, 0, half // 4)
    rows_down.wait_recv()
    charge_down.wait_recv()
    charge_above = charge_next[0:1, :]

    def cross_step(step, total):
        flat = unpack(packed_ref[rows_of(step), :], odd_rows(step, charge))
        other = unpack(packed_next[rows_of(step), :], odd_rows(step, charge_above))
        return total + lax.dot_general(flat, other, (((0,), (0,)), ((), ())), preferred_element_type=jnp.float32)

    cross = lax.fori_loop(0, tiles, cross_step, jnp.zeros((bond, bond), jnp.float32))
    cross_part[: count // 2] = cross[:, :half].reshape(count // 2, -1, half)
    cross_part[count // 2 :] = cross[:, half:].reshape(count // 2, -1, half)

    @pl.loop(1, count)
    def _(k):
        scatter(k, cross_part, cross_land, send_c, recv_c).start()

    cross_land[0] = cross_part[me]
    invert_factor(state, half, half // 4, half)
    inverse_down = to_below(state, inverse_next, 2)
    inverse_down.start()

    @pl.loop(1, count)
    def _(k):
        scatter(k, cross_part, cross_land, send_c, recv_c).wait_recv()

    cross_all[me] = jnp.sum(cross_land[...], axis=0)

    @pl.loop(1, count)
    def _(k):
        gather(k, me, cross_all, send_d, recv_d).start()

    own = jnp.concatenate([state[0].T, state[1].T], axis=1)

    @pl.loop(0, tiles)
    def _(step):
        out = exact_dot(packed_ref[rows_of(step), :], own)
        out_ref[rows_of(step), :] = mask_halves(out, odd_rows(step, charge))

    inverse_down.wait_recv()
    following = jnp.concatenate([inverse_next[0].T, inverse_next[1].T], axis=1)
    next_rows = packed_next.reshape(phys, bond, half)
    spot = lax.broadcasted_iota(jnp.int32, (block, half), 0)

    @pl.loop(0, bond // group)
    def _(step):
        left = pl.ds(pl.multiple_of(step * group, group), group)
        rows = jnp.swapaxes(next_rows[:, left, :].astype(jnp.float32), 0, 1).reshape(block, half)
        odd = ((step * group + spot // phys) >= charge_above) != (lax.rem(spot, phys) >= phys // 2)
        out = exact_dot(rows.astype(jnp.bfloat16), following)
        compressed_next[pl.ds(pl.multiple_of(step * block, block), block), :] = mask_halves(out, odd)

    @pl.loop(1, count)
    def _(k):
        gather(k, before(k), cross_all, send_d, recv_d).wait_recv()

    total = jnp.concatenate(
        [cross_all[: count // 2].reshape(bond, half), cross_all[count // 2 :].reshape(bond, half)], axis=1
    )
    upper = jnp.concatenate(
        [
            jnp.dot(state[0], total[:half], precision=HIGH, preferred_element_type=jnp.float32),
            jnp.dot(state[1], total[half:], precision=HIGH, preferred_element_type=jnp.float32),
        ],
        axis=0,
    )
    turn = (((1,), (1,)), ((), ()))
    correlation = jnp.concatenate(
        [
            lax.dot_general(upper[:, :half], inverse_next[0], turn, precision=HIGH, preferred_element_type=jnp.float32),
            lax.dot_general(upper[:, half:], inverse_next[1], turn, precision=HIGH, preferred_element_type=jnp.float32),
        ],
        axis=1,
    )
    mixing = (correlation * mix_scale).T.astype(jnp.bfloat16)

    def gradient_step(step, total):
        rows = pl.ds(pl.multiple_of(step * block, block), block)
        adjoint = jnp.dot(compressed_next[rows, :], mixing, preferred_element_type=jnp.float32).astype(jnp.bfloat16)
        return total + lax.dot_general(adjoint, ordered[rows, :], turn, preferred_element_type=jnp.float32)

    pairs = lax.fori_loop(0, bond // group, gradient_step, jnp.zeros((block, block), jnp.float32))
    down = lax.broadcasted_iota(jnp.int32, (block, block), 0)
    across = lax.broadcasted_iota(jnp.int32, (block, block), 1)
    pairs = jnp.where(down // phys == across // phys, pairs, 0.0).reshape(group, phys, block).sum(axis=0)
    tall = lax.broadcasted_iota(jnp.int32, (block, phys), 0)
    wide = lax.broadcasted_iota(jnp.int32, (block, phys), 1)
    fold = jnp.where(lax.rem(tall, phys) == wide, 1.0, 0.0)
    gradient = jnp.dot(pairs, fold, precision=HIGH, preferred_element_type=jnp.float32)
    grad_ref[...] = jnp.where(row == sections - 1, 0.0, gradient / bond)
    rows_down.wait_send()
    charge_down.wait_send()
    inverse_down.wait_send()

    @pl.loop(1, count)
    def _(k):
        scatter(k, gram_part, gram_land, send_a, recv_a).wait_send()
        gather(k, me, gram_all, send_b, recv_b).wait_send()
        scatter(k, cross_part, cross_land, send_c, recv_c).wait_send()
        gather(k, me, cross_all, send_d, recv_d).wait_send()


def shards(boundary_in, row_operator, charges):
    stored, oper, charge = boundary_in[0, 0], row_operator[0, 0], charges[0, 0]
    phys, bond = stored.shape[0], stored.shape[2]
    half, phalf = bond // 2, phys // 2
    count, sections = lax.axis_size("cols"), lax.axis_size("rows")
    left_odd = (jnp.arange(bond) >= charge)[None, :, None]
    low, high = stored[:, :, :half], stored[:, :, half:]
    applied = jnp.concatenate(
        [
            jnp.einsum("pq,qlc->plc", oper[:phalf], jnp.where(left_odd, high, low), preferred_element_type=jnp.float32),
            jnp.einsum("pq,qlc->plc", oper[phalf:], jnp.where(left_odd, low, high), preferred_element_type=jnp.float32),
        ]
    )
    packed = applied.astype(jnp.bfloat16).reshape(-1, half)
    scale = 2.0 / (count * phys * bond)
    mix_scale = 2.0 / (bond * math.sqrt(count * phys))
    vmem = pl.BlockSpec(memory_space=pltpu.VMEM)
    gram_shape = (count, half * bond // count // half, half)
    cross_shape = (count, bond * bond // count // half, half)
    sems = pltpu.SemaphoreType.DMA((count,))
    compressed, gradient = pl.pallas_call(
        functools.partial(whole_kernel, count, sections, phys, bond, scale, mix_scale),
        out_shape=(
            jax.ShapeDtypeStruct((phys * bond, bond), jnp.bfloat16),
            jax.ShapeDtypeStruct((phys, phys), jnp.float32),
        ),
        in_specs=[vmem, pl.BlockSpec(memory_space=pl.ANY), pl.BlockSpec(memory_space=pltpu.SMEM)],
        out_specs=(vmem, vmem),
        scratch_shapes=[
            pltpu.VMEM((phys, bond, bond), jnp.bfloat16),
            pltpu.VMEM((phys * bond, bond), jnp.bfloat16),
            pltpu.VMEM((phys * bond, half), jnp.bfloat16),
            pltpu.VMEM((phys * bond, bond), jnp.bfloat16),
            pltpu.VMEM((8, half), jnp.int32),
            pltpu.VMEM((8, half), jnp.int32),
            pltpu.VMEM((2, half, half), jnp.float32),
            pltpu.VMEM((2, half, half), jnp.float32),
            pltpu.VMEM(gram_shape, jnp.float32),
            pltpu.VMEM(gram_shape, jnp.float32),
            pltpu.VMEM(gram_shape, jnp.float32),
            pltpu.VMEM(cross_shape, jnp.float32),
            pltpu.VMEM(cross_shape, jnp.float32),
            pltpu.VMEM(cross_shape, jnp.float32),
            sems, sems, sems, sems, sems, sems, sems, sems,
            pltpu.SemaphoreType.DMA((3,)),
            pltpu.SemaphoreType.DMA((3,)),
            pltpu.SemaphoreType.DMA,
        ],
        compiler_params=pltpu.CompilerParams(collective_id=0, has_side_effects=True),
        name="orthonormalise",
    )(packed, stored, charges)
    return (compressed.reshape(boundary_in.shape), gradient[None, None])


def solution(mesh):
    return jax.shard_map(
        shards,
        mesh=mesh,
        in_specs=(
            P("rows", "cols", None, None, None),
            P("rows", "cols", None, None),
            P("rows", "cols"),
        ),
        out_specs=(P("rows", "cols", None, None, None), P("rows", "cols", None, None)),
        check_vma=False,
    )
```

time: 130 us -> 72.2 us (0.56)
  other arithmetic: 52.7 us -> 1.95 us
  Pallas kernels: 43.1 us -> 61.3 us
  matrix products: 15.1 us -> 1.33 us
  local copies, waits for them, and re-layouts: 11.1 us -> 4.95 us
  starting transfers between devices: 4.06 us -> 0 us
    another operation x8 -> x0, other arithmetic: 43.4 us -> none  [the longest x4 23.6 us: shards(): factor = jnp.linalg.cholesky(grams)]
    pallas_call x2 -> x1, Pallas kernels: 43.1 us -> 61.3 us  [shards(): pl.pallas_call(functools.partial(whole_kernel, count, sections, phys, bon...]
    dot_general x8 -> x0, matrix products: 13.4 us -> none  [the longest x2 6.8 us: compress(): jnp.dot(rows, both, precision=HIGH, preferred_element_type=jnp.float32)]
    select_n x2 -> x0, other arithmetic: 5.68 us -> none  [unpack(): jnp.where(odd, zero, packed)]
    reshape x4 -> x0, local copies, waits for them, and re-layouts: 5.55 us -> none  [the longest x1 3.14 us: shards(): adjoint = adjoint.reshape(phys_dim, bond_dim, bond_dim)]
    ppermute x3 -> x0, starting transfers between devices: 4.06 us -> none  [from_next(): return lax.ppermute(value, 'rows', [(r + 1, r) for r in range(count - 1)])]
    squeeze x3 -> x0, local copies, waits for them, and re-layouts: 3.15 us -> none  [the longest x1 3.11 us: shards(): boundary_in[0, 0]]
    unnamed x14 -> x6, local copies, waits for them, and re-layouts: 1.96 us -> 3.71 us
  transfers between devices with their start and end apart: 3 -> 0, of which waited for: 0 -> 0; matrix products, arithmetic and copies ran while one was open for 51% -> 0% of each run, Pallas kernels for 18% -> 0%
where the time goes in v3:
time: 72.2 us; the launch traced here: 70.8 us
  Pallas kernels  61.3 us (85%)
  local copies, waits for them, and re-layouts  4.95 us (7%)
  other arithmetic  1.95 us (3%)
  between operations  1.34 us (2%)
  matrix products  1.33 us (2%)
    pallas_call x1, Pallas kernels, shards(): pl.pallas_call(functools.partial(whole_kernel, count, sections, phys, bon...  61.3 us
    unnamed x6, local copies, waits for them, and re-layouts  3.71 us
    select_n x1, other arithmetic, shards(): jnp.where(left_odd, high, low)  1.76 us

profile of v3, /device:TPU:1, one launch (start us, length us, event | category | flops | bytes accessed | tf_op | source)
XLA Modules:
  0.0 70.8 jit_solution(5287529447312579369)
XLA Ops:
  1.3 0.0 copy-start.1
  1.3 1.8 %broadcast_select_fusion.1 = (bf16[16,256,128]{2,1,0:T(8,128)(2,1)S(1)}, bf16[16,256,128]{2,1,0:T(8,128)(2,1)S(1)}) fusion(pred[256]{0:T(512)(128)(4,1)S(1)} %iota_compare_fusion, bf16[16,256,256]{2,1,0:T(8,128)(2,1)} %bitcast.20), kind=kLoop, calls=%fused_computation.8 | loop fusion | flops 1048576 | bytes 4194560 | tf_op jit(solution)/shard_map/jit(_where)/select_n | solution.py:302
  3.1 0.0 copy-done.1
  3.1 0.7 fusion
  3.7 0.7 fusion.1
  4.4 0.2 pad_maximum_fusion
  4.6 1.2 %copy.7 = bf16[16,256,128]{2,1,0:T(8,128)(2,1)} copy(bf16[16,256,128]{2,0,1:T(8,128)(2,1)S(1)} %pad_maximum_fusion) | data formatting | bytes 2097152 | tf_op jit(solution)/shard_map/concatenate | solution.py:300
  5.9 61.3 %orthonormalise.1 = (bf16[4096,256]{1,0:T(8,128)(2,1)}, f32[16,16]{1,0:T(8,128)}) custom-call(bf16[4096,128]{1,0:T(8,128)(2,1)} %bitcast.22, bf16[16,256,256]{2,1,0:T(8,128)(2,1)} %bitcast.21, s32[1,1]{1,0:T(1,128)} %copy.14.charge_ref), custom_call_target="tpu_custom_call" | custom-call | tf_op jit(solution)/shard_map/orthonormalise/pallas_call | solution.py:313
  67.1 0.0 copy-start
  67.1 3.1 %copy.15 = bf16[1,1,16,256,256]{4,3,2,1,0:T(8,128)(2,1)} copy(bf16[1,1,16,256,256]{4,3,2,1,0:T(8,128)(2,1)} %bitcast.23) | data formatting | bytes 4194304
  70.2 0.0 copy-done
  70.2 0.6 copy.16
  (1 shorter events, 0.0 us)
Async XLA Ops:
  1.3 1.8 %copy-start.1 = (bf16[1,1,16,16]{3,2,1,0:T(8,128)(2,1)S(1)}, bf16[1,1,16,16]{3,2,1,0:T(8,128)(2,1)}, u32[]{:S(2)}) copy-start(bf16[1,1,16,16]{3,2,1,0:T(8,128)(2,1)} %param.4) | copy-start | bytes 1540
  67.1 3.1 %copy-start = (f32[16,16]{1,0:T(8,128)S(1)}, f32[16,16]{1,0:T(8,128)}, u32[]{:S(2)}) copy-start(f32[16,16]{1,0:T(8,128)} %get-tuple-element.5) | copy-start | bytes 3076

commit v4 on v3

--- a/solution.py
+++ b/solution.py
@@ -54,12 +54,14 @@
             state[b, base:stop, :] = jnp.where(lane <= sub + base, done * lax.rsqrt(pivots), 0.0)
 
 
-def exact_dot(rows, weights):
+def exact_parts(weights):
     high, mid, low = split3(weights)
-    pair = jnp.concatenate([high, mid], axis=0).astype(jnp.bfloat16)
-    twice = jnp.concatenate([rows, rows], axis=1)
-    out = jnp.dot(twice, pair, preferred_element_type=jnp.float32)
-    return out + jnp.dot(rows, low.astype(jnp.bfloat16), preferred_element_type=jnp.float32)
+    return jnp.concatenate([high, mid], axis=0).astype(jnp.bfloat16), low.astype(jnp.bfloat16)
+
+
+def exact_dot(rows, parts):
+    out = jnp.dot(jnp.concatenate([rows, rows], axis=1), parts[0], preferred_element_type=jnp.float32)
+    return out + jnp.dot(rows, parts[1], preferred_element_type=jnp.float32)
 
 
 def unpack(rows, odd):
@@ -74,11 +76,11 @@
 
 def whole_kernel(
     count, sections, phys, bond, scale, mix_scale,
-    packed_ref, stored_hbm, charge_ref,
-    out_ref, grad_ref,
-    stored, ordered, packed_next, compressed_next, charge_own, charge_next,
+    even_ref, other_ref, stored_hbm, charge_ref,
+    out_hbm, grad_ref,
+    stored, ordered, packed_next, compressed_next, turned, adjoints, out, charge_own, charge_next,
     state, inverse_next, gram_part, gram_land, gram_all, cross_part, cross_land, cross_all,
-    send_a, recv_a, send_b, recv_b, send_c, recv_c, send_d, recv_d, send_r, recv_r, load_sem,
+    send_a, recv_a, send_b, recv_b, send_c, recv_c, send_d, recv_d, send_r, recv_r, load_sem, store_sem,
 ):
     me = lax.axis_index("cols")
     row = lax.axis_index("rows")
@@ -113,18 +115,11 @@
         phys_odd = (2 * step + place // bond) >= phys // 2
         return left_odd != phys_odd
 
+    packed = (even_ref, other_ref)
+    per_half = tiles // 2
+
     def rows_of(step):
         return pl.ds(pl.multiple_of(step * tile, tile), tile)
-
-    def gram_step(step, total):
-        rows = packed_ref[rows_of(step), :]
-        flat = unpack(rows, odd_rows(step, charge))
-        return total + lax.dot_general(rows, flat, (((0,), (0,)), ((), ())), preferred_element_type=jnp.float32)
-
-    gram = lax.fori_loop(0, tiles, gram_step, jnp.zeros((half, bond), jnp.float32))
-    gram_part[: count // 2] = gram[:, :half].reshape(count // 2, -1, half)
-    gram_part[count // 2 :] = gram[:, half:].reshape(count // 2, -1, half)
-    pl.semaphore_wait(barrier, count + 1)
 
     def to_below(source, target, index):
         return pltpu.make_async_remote_copy(
@@ -132,6 +127,37 @@
             device_id={"rows": below}, device_id_type=MESH,
         )
 
+    pieces = 4
+    piece = phys * bond // pieces
+    charge_down = to_below(charge_own, charge_next, pieces)
+    rows_down = []
+    for index in range(pieces):
+        start = index * piece % (pieces // 2 * piece)
+        source = packed[index * 2 // pieces].at[start : start + piece, :]
+        rows_down.append(to_below(source, packed_next.at[index * piece : (index + 1) * piece, :], index))
+    pl.semaphore_wait(barrier, count + 1)
+    charge_down.start()
+    for copy in rows_down:
+        copy.start()
+    lane_place = lax.broadcasted_iota(jnp.int32, (half, tile), 1)
+    gram = jnp.zeros((half, bond), jnp.float32)
+    for which in range(2):
+
+        def gram_step(step, total, which=which):
+            rows = packed[which][rows_of(step), :]
+            across = rows.T
+            flat = unpack(rows, odd_rows(which * per_half + step, charge))
+            wide = across.astype(jnp.float32)
+            odd = (lax.rem(lane_place, bond) >= charge) != (which == 1)
+            columns = rows_of(which * per_half + step)
+            turned[:half, columns] = jnp.where(odd, 0.0, wide).astype(jnp.bfloat16)
+            turned[half:, columns] = jnp.where(odd, wide, 0.0).astype(jnp.bfloat16)
+            return total + jnp.dot(across, flat, preferred_element_type=jnp.float32)
+
+        gram = lax.fori_loop(0, per_half, gram_step, gram)
+    gram_part[: count // 2] = gram[:, :half].reshape(count // 2, -1, half)
+    gram_part[count // 2 :] = gram[:, half:].reshape(count // 2, -1, half)
+
     def scatter(k, part, land, send, recv):
         return pltpu.make_async_remote_copy(
             src_ref=part.at[after(k)], dst_ref=land.at[k], send_sem=send.at[k], recv_sem=recv.at[k],
@@ -148,10 +174,6 @@
     def _(k):
         scatter(k, gram_part, gram_land, send_a, recv_a).start()
 
-    rows_down = to_below(packed_ref, packed_next, 0)
-    rows_down.start()
-    charge_down = to_below(charge_own, charge_next, 1)
-    charge_down.start()
     gram_land[0] = gram_part[me]
     load.wait()
     group = bond // phys
@@ -161,7 +183,7 @@
         left = pl.ds(pl.multiple_of(step * group, group), group)
         rows = source[:, left, :].astype(jnp.float32)
         rows = jnp.swapaxes(rows, 0, 1).reshape(block, rows.shape[2])
-        target[pl.ds(pl.multiple_of(step * block, block), block), :] = rows.astype(jnp.bfloat16)
+        target[pl.ds(pl.multiple_of(step * bond, bond), bond), :] = rows.T.astype(jnp.bfloat16)
 
     @pl.loop(0, bond // group // 2)
     def _(step):
@@ -187,17 +209,23 @@
 
     state[0] = gram_all[: count // 2].reshape(half, half) * scale
     state[1] = gram_all[count // 2 :].reshape(half, half) * scale
-    invert_factor(state, half, 0, half // 4)
-    rows_down.wait_recv()
+    invert_factor(state, half, 0, half)
+    inverse_down = to_below(state, inverse_next, pieces + 1)
+    inverse_down.start()
     charge_down.wait_recv()
     charge_above = charge_next[0:1, :]
-
-    def cross_step(step, total):
-        flat = unpack(packed_ref[rows_of(step), :], odd_rows(step, charge))
-        other = unpack(packed_next[rows_of(step), :], odd_rows(step, charge_above))
-        return total + lax.dot_general(flat, other, (((0,), (0,)), ((), ())), preferred_element_type=jnp.float32)
-
-    cross = lax.fori_loop(0, tiles, cross_step, jnp.zeros((bond, bond), jnp.float32))
+    cross = jnp.zeros((bond, bond), jnp.float32)
+    for index in range(pieces):
+        rows_down[index].wait_recv()
+        first = index * piece // tile
+        other = jnp.concatenate(
+            [
+                unpack(packed_next[step * tile : (step + 1) * tile, :], odd_rows(step, charge_above))
+                for step in range(first, first + piece // tile)
+            ],
+            axis=0,
+        )
+        cross += jnp.dot(turned[:, index * piece : (index + 1) * piece], other, preferred_element_type=jnp.float32)
     cross_part[: count // 2] = cross[:, :half].reshape(count // 2, -1, half)
     cross_part[count // 2 :] = cross[:, half:].reshape(count // 2, -1, half)
 
@@ -206,9 +234,17 @@
         scatter(k, cross_part, cross_land, send_c, recv_c).start()
 
     cross_land[0] = cross_part[me]
-    invert_factor(state, half, half // 4, half)
-    inverse_down = to_below(state, inverse_next, 2)
-    inverse_down.start()
+    own = exact_parts(jnp.concatenate([state[0].T, state[1].T], axis=1))
+    for which in range(2):
+
+        @pl.loop(0, per_half)
+        def _(step, which=which):
+            wide = exact_dot(packed[which][rows_of(step), :], own)
+            step = which * per_half + step
+            out[rows_of(step), :] = mask_halves(wide, odd_rows(step, charge))
+
+    store = pltpu.make_async_copy(out, out_hbm, store_sem)
+    store.start()
 
     @pl.loop(1, count)
     def _(k):
@@ -220,15 +256,8 @@
     def _(k):
         gather(k, me, cross_all, send_d, recv_d).start()
 
-    own = jnp.concatenate([state[0].T, state[1].T], axis=1)
-
-    @pl.loop(0, tiles)
-    def _(step):
-        out = exact_dot(packed_ref[rows_of(step), :], own)
-        out_ref[rows_of(step), :] = mask_halves(out, odd_rows(step, charge))
-
     inverse_down.wait_recv()
-    following = jnp.concatenate([inverse_next[0].T, inverse_next[1].T], axis=1)
+    following = exact_parts(jnp.concatenate([inverse_next[0].T, inverse_next[1].T], axis=1))
     next_rows = packed_next.reshape(phys, bond, half)
     spot = lax.broadcasted_iota(jnp.int32, (block, half), 0)
 
@@ -237,8 +266,8 @@
         left = pl.ds(pl.multiple_of(step * group, group), group)
         rows = jnp.swapaxes(next_rows[:, left, :].astype(jnp.float32), 0, 1).reshape(block, half)
         odd = ((step * group + spot // phys) >= charge_above) != (lax.rem(spot, phys) >= phys // 2)
-        out = exact_dot(rows.astype(jnp.bfloat16), following)
-        compressed_next[pl.ds(pl.multiple_of(step * block, block), block), :] = mask_halves(out, odd)
+        wide = exact_dot(rows.astype(jnp.bfloat16), following)
+        compressed_next[pl.ds(pl.multiple_of(step * block, block), block), :] = mask_halves(wide, odd)
 
     @pl.loop(1, count)
     def _(k):
@@ -264,12 +293,13 @@
     )
     mixing = (correlation * mix_scale).T.astype(jnp.bfloat16)
 
-    def gradient_step(step, total):
-        rows = pl.ds(pl.multiple_of(step * block, block), block)
-        adjoint = jnp.dot(compressed_next[rows, :], mixing, preferred_element_type=jnp.float32).astype(jnp.bfloat16)
-        return total + lax.dot_general(adjoint, ordered[rows, :], turn, preferred_element_type=jnp.float32)
-
-    pairs = lax.fori_loop(0, bond // group, gradient_step, jnp.zeros((block, block), jnp.float32))
+    for step in range(pieces):
+        mixed = jnp.dot(compressed_next[step * piece : (step + 1) * piece, :], mixing, preferred_element_type=jnp.float32)
+        mixed = mixed.astype(jnp.bfloat16)
+        for part in range(piece // block):
+            column = (step * (piece // block) + part) * bond
+            adjoints[:, column : column + bond] = mixed[part * block : (part + 1) * block]
+    pairs = jnp.dot(adjoints[...], ordered[...], preferred_element_type=jnp.float32)
     down = lax.broadcasted_iota(jnp.int32, (block, block), 0)
     across = lax.broadcasted_iota(jnp.int32, (block, block), 1)
     pairs = jnp.where(down // phys == across // phys, pairs, 0.0).reshape(group, phys, block).sum(axis=0)
@@ -278,9 +308,11 @@
     fold = jnp.where(lax.rem(tall, phys) == wide, 1.0, 0.0)
     gradient = jnp.dot(pairs, fold, precision=HIGH, preferred_element_type=jnp.float32)
     grad_ref[...] = jnp.where(row == sections - 1, 0.0, gradient / bond)
-    rows_down.wait_send()
+    for copy in rows_down:
+        copy.wait_send()
     charge_down.wait_send()
     inverse_down.wait_send()
+    store.wait()
 
     @pl.loop(1, count)
     def _(k):
@@ -297,13 +329,10 @@
     count, sections = lax.axis_size("cols"), lax.axis_size("rows")
     left_odd = (jnp.arange(bond) >= charge)[None, :, None]
     low, high = stored[:, :, :half], stored[:, :, half:]
-    applied = jnp.concatenate(
-        [
-            jnp.einsum("pq,qlc->plc", oper[:phalf], jnp.where(left_odd, high, low), preferred_element_type=jnp.float32),
-            jnp.einsum("pq,qlc->plc", oper[phalf:], jnp.where(left_odd, low, high), preferred_element_type=jnp.float32),
-        ]
-    )
-    packed = applied.astype(jnp.bfloat16).reshape(-1, half)
+    even = jnp.einsum("pq,qlc->plc", oper[:phalf], jnp.where(left_odd, high, low), preferred_element_type=jnp.float32)
+    other = jnp.einsum("pq,qlc->plc", oper[phalf:], jnp.where(left_odd, low, high), preferred_element_type=jnp.float32)
+    even = even.astype(jnp.bfloat16).reshape(-1, half)
+    other = other.astype(jnp.bfloat16).reshape(-1, half)
     scale = 2.0 / (count * phys * bond)
     mix_scale = 2.0 / (bond * math.sqrt(count * phys))
     vmem = pl.BlockSpec(memory_space=pltpu.VMEM)
@@ -316,12 +345,15 @@
             jax.ShapeDtypeStruct((phys * bond, bond), jnp.bfloat16),
             jax.ShapeDtypeStruct((phys, phys), jnp.float32),
         ),
-        in_specs=[vmem, pl.BlockSpec(memory_space=pl.ANY), pl.BlockSpec(memory_space=pltpu.SMEM)],
-        out_specs=(vmem, vmem),
+        in_specs=[vmem, vmem, pl.BlockSpec(memory_space=pl.ANY), pl.BlockSpec(memory_space=pltpu.SMEM)],
+        out_specs=(pl.BlockSpec(memory_space=pl.ANY), vmem),
         scratch_shapes=[
             pltpu.VMEM((phys, bond, bond), jnp.bfloat16),
             pltpu.VMEM((phys * bond, bond), jnp.bfloat16),
             pltpu.VMEM((phys * bond, half), jnp.bfloat16),
+            pltpu.VMEM((phys * bond, bond), jnp.bfloat16),
+            pltpu.VMEM((bond, phys * bond), jnp.bfloat16),
+            pltpu.VMEM((bond, phys * bond), jnp.bfloat16),
             pltpu.VMEM((phys * bond, bond), jnp.bfloat16),
             pltpu.VMEM((8, half), jnp.int32),
             pltpu.VMEM((8, half), jnp.int32),
@@ -334,13 +366,14 @@
             pltpu.VMEM(cross_shape, jnp.float32),
             pltpu.VMEM(cross_shape, jnp.float32),
             sems, sems, sems, sems, sems, sems, sems, sems,
-            pltpu.SemaphoreType.DMA((3,)),
-            pltpu.SemaphoreType.DMA((3,)),
+            pltpu.SemaphoreType.DMA((6,)),
+            pltpu.SemaphoreType.DMA((6,)),
+            pltpu.SemaphoreType.DMA,
             pltpu.SemaphoreType.DMA,
         ],
         compiler_params=pltpu.CompilerParams(collective_id=0, has_side_effects=True),
         name="orthonormalise",
-    )(packed, stored, charges)
+    )(even, other, stored, charges)
     return (compressed.reshape(boundary_in.shape), gradient[None, None])
 
 

time: 72.2 us -> 63.2 us (0.88); the launches traced: 70.8 us -> 62.9 us
  Pallas kernels: 61.3 us -> 53 us
    pallas_call x1, Pallas kernels: 61.3 us -> 53 us  [shards(): pl.pallas_call(functools.partial(whole_kernel, count, sections, phys, bon...]
    convert_element_type x0 -> x2, local copies, waits for them, and re-layouts: none -> 1.77 us  [the longest x1 0.89 us: shards(): even = even.astype(jnp.bfloat16).reshape(-1, half)]
    concatenate x1 -> x0, local copies, waits for them, and re-layouts: 1.24 us -> none  [shards(): jnp.concatenate([jnp.einsum('pq,qlc->plc', oper[:phalf], jnp.where(left_o...]
where the time goes in v4:
time: 63.2 us; the launch traced here: 62.9 us
  Pallas kernels  53 us (84%)
  local copies, waits for them, and re-layouts  5.48 us (9%)
  other arithmetic  1.77 us (3%)
  matrix products  1.33 us (2%)
  between operations  1.33 us (2%)
    pallas_call x1, Pallas kernels, shards(): pl.pallas_call(functools.partial(whole_kernel, count, sections, phys, bon...  53 us
    unnamed x6, local copies, waits for them, and re-layouts  3.71 us
    select_n x1, other arithmetic, shards(): jnp.where(left_odd, low, high)  1.76 us

profile of v4, /device:TPU:1, one launch (start us, length us, event | category | flops | bytes accessed | tf_op | source)
XLA Modules:
  0.0 62.9 jit_solution(17216606304665804273)
XLA Ops:
  1.3 0.0 copy-start.1
  1.3 1.8 %broadcast_select_fusion = (bf16[16,256,128]{2,1,0:T(8,128)(2,1)S(1)}, bf16[16,256,128]{2,1,0:T(8,128)(2,1)S(1)}) fusion(pred[256]{0:T(512)(128)(4,1)S(1)} %iota_compare_fusion, bf16[16,256,256]{2,1,0:T(8,128)(2,1)} %bitcast.21), kind=kLoop, calls=%fused_computation.6 | loop fusion | flops 1048576 | bytes 4194560 | tf_op jit(solution)/shard_map/jit(_where)/select_n | solution.py:333
  3.1 0.0 copy-done.1
  3.1 0.7 %fusion.1 = bf16[8,256,128]{2,0,1:T(8,128)(2,1)S(1)} fusion(bf16[16,256,128]{2,1,0:T(8,128)(2,1)S(1)} %get-tuple-element.6, bf16[1,1,16,16]{3,2,1,0:T(8,128)(2,1)S(1)} %copy-done.1), kind=kOutput, calls=%fused_computation.3 | convolution fusion | flops 8650752 | bytes 1574912 | tf_op jit(solution)/shard_map/pq,qlc->plc/dot_general | solution.py:333
  3.7 0.7 %fusion = bf16[8,256,128]{2,0,1:T(8,128)(2,1)S(1)} fusion(bf16[16,256,128]{2,1,0:T(8,128)(2,1)S(1)} %get-tuple-element.7, bf16[1,1,16,16]{3,2,1,0:T(8,128)(2,1)S(1)} %copy-done.1), kind=kOutput, calls=%fused_computation.2 | convolution fusion | flops 8650752 | bytes 1574912 | tf_op jit(solution)/shard_map/pq,qlc->plc/dot_general | solution.py:332
  4.4 0.9 %copy.6 = bf16[8,256,128]{2,1,0:T(8,128)(2,1)} copy(bf16[8,256,128]{2,0,1:T(8,128)(2,1)S(1)} %fusion) | data formatting | bytes 1048576 | tf_op jit(solution)/shard_map/convert_element_type | solution.py:334
  5.3 0.9 %copy.8 = bf16[8,256,128]{2,1,0:T(8,128)(2,1)} copy(bf16[8,256,128]{2,0,1:T(8,128)(2,1)S(1)} %fusion.1) | data formatting | bytes 1048576 | tf_op jit(solution)/shard_map/convert_element_type | solution.py:335
  6.2 53.0 %orthonormalise.1 = (bf16[4096,256]{1,0:T(8,128)(2,1)}, f32[16,16]{1,0:T(8,128)}) custom-call(bf16[2048,128]{1,0:T(8,128)(2,1)} %bitcast.24, bf16[2048,128]{1,0:T(8,128)(2,1)} %bitcast.25, bf16[16,256,256]{2,1,0:T(8,128)(2,1)} %bitcast.22, s32[1,1]{1,0:T(1,128)} %copy.15.charge_ref), custom_call_target="tpu_custom_call" | custom-call | tf_op jit(solution)/shard_map/orthonormalise/pallas_call | solution.py:342
  59.2 0.0 copy-start
  59.2 3.1 %copy.16 = bf16[1,1,16,256,256]{4,3,2,1,0:T(8,128)(2,1)} copy(bf16[1,1,16,256,256]{4,3,2,1,0:T(8,128)(2,1)} %bitcast.23) | data formatting | bytes 4194304
  62.3 0.0 copy-done
  62.3 0.6 copy.17
  (1 shorter events, 0.0 us)
Async XLA Ops:
  1.3 1.8 %copy-start.1 = (bf16[1,1,16,16]{3,2,1,0:T(8,128)(2,1)S(1)}, bf16[1,1,16,16]{3,2,1,0:T(8,128)(2,1)}, u32[]{:S(2)}) copy-start(bf16[1,1,16,16]{3,2,1,0:T(8,128)(2,1)} %param.4) | copy-start | bytes 1540
  59.2 3.1 %copy-start = (f32[16,16]{1,0:T(8,128)S(1)}, f32[16,16]{1,0:T(8,128)}, u32[]{:S(2)}) copy-start(f32[16,16]{1,0:T(8,128)} %get-tuple-element.5) | copy-start | bytes 3076

commit v5 on v4

--- a/solution.py
+++ b/solution.py
@@ -110,10 +110,12 @@
     tiles = phys // 2
     place = lax.broadcasted_iota(jnp.int32, (tile, half), 0)
 
-    def odd_rows(step, charge):
-        left_odd = lax.rem(place, bond) >= charge
-        phys_odd = (2 * step + place // bond) >= phys // 2
-        return left_odd != phys_odd
+    phalf = phys // 2
+    lefts = tile // phalf
+
+    def odd_rows(which, step, charge):
+        left_odd = (step * lefts + place // phalf) >= charge
+        return left_odd != (which == 1)
 
     packed = (even_ref, other_ref)
     per_half = tiles // 2
@@ -146,9 +148,9 @@
         def gram_step(step, total, which=which):
             rows = packed[which][rows_of(step), :]
             across = rows.T
-            flat = unpack(rows, odd_rows(which * per_half + step, charge))
+            flat = unpack(rows, odd_rows(which, step, charge))
             wide = across.astype(jnp.float32)
-            odd = (lax.rem(lane_place, bond) >= charge) != (which == 1)
+            odd = ((step * lefts + lane_place // phalf) >= charge) != (which == 1)
             columns = rows_of(which * per_half + step)
             turned[:half, columns] = jnp.where(odd, 0.0, wide).astype(jnp.bfloat16)
             turned[half:, columns] = jnp.where(odd, wide, 0.0).astype(jnp.bfloat16)
@@ -220,7 +222,7 @@
         first = index * piece // tile
         other = jnp.concatenate(
             [
-                unpack(packed_next[step * tile : (step + 1) * tile, :], odd_rows(step, charge_above))
+                unpack(packed_next[step * tile : (step + 1) * tile, :], odd_rows(step // per_half, step % per_half, charge_above))
                 for step in range(first, first + piece // tile)
             ],
             axis=0,
@@ -240,8 +242,10 @@
         @pl.loop(0, per_half)
         def _(step, which=which):
             wide = exact_dot(packed[which][rows_of(step), :], own)
-            step = which * per_half + step
-            out[rows_of(step), :] = mask_halves(wide, odd_rows(step, charge))
+            wide = mask_halves(wide, odd_rows(which, step, charge)).astype(jnp.float32)
+            wide = jnp.swapaxes(wide.reshape(lefts, phalf, bond), 0, 1)
+            left = pl.ds(pl.multiple_of(step * lefts, lefts), lefts)
+            out[which * phalf : (which + 1) * phalf, left, :] = wide.astype(jnp.bfloat16)
 
     store = pltpu.make_async_copy(out, out_hbm, store_sem)
     store.start()
@@ -258,16 +262,13 @@
 
     inverse_down.wait_recv()
     following = exact_parts(jnp.concatenate([inverse_next[0].T, inverse_next[1].T], axis=1))
-    next_rows = packed_next.reshape(phys, bond, half)
-    spot = lax.broadcasted_iota(jnp.int32, (block, half), 0)
-
-    @pl.loop(0, bond // group)
-    def _(step):
-        left = pl.ds(pl.multiple_of(step * group, group), group)
-        rows = jnp.swapaxes(next_rows[:, left, :].astype(jnp.float32), 0, 1).reshape(block, half)
-        odd = ((step * group + spot // phys) >= charge_above) != (lax.rem(spot, phys) >= phys // 2)
-        wide = exact_dot(rows.astype(jnp.bfloat16), following)
-        compressed_next[pl.ds(pl.multiple_of(step * block, block), block), :] = mask_halves(wide, odd)
+    for which in range(2):
+
+        @pl.loop(0, per_half)
+        def _(step, which=which):
+            rows = rows_of(which * per_half + step)
+            wide = exact_dot(packed_next[rows, :], following)
+            compressed_next[rows, :] = mask_halves(wide, odd_rows(which, step, charge_above))
 
     @pl.loop(1, count)
     def _(k):
@@ -296,13 +297,17 @@
     for step in range(pieces):
         mixed = jnp.dot(compressed_next[step * piece : (step + 1) * piece, :], mixing, preferred_element_type=jnp.float32)
         mixed = mixed.astype(jnp.bfloat16)
-        for part in range(piece // block):
-            column = (step * (piece // block) + part) * bond
-            adjoints[:, column : column + bond] = mixed[part * block : (part + 1) * block]
+        which, place_in_half = divmod(step, pieces // 2)
+        height = block // 2
+        for part in range(piece // height):
+            column = (place_in_half * (piece // height) + part) * bond
+            chunk = mixed[part * height : (part + 1) * height]
+            adjoints[which * height : (which + 1) * height, column : column + bond] = chunk
     pairs = jnp.dot(adjoints[...], ordered[...], preferred_element_type=jnp.float32)
     down = lax.broadcasted_iota(jnp.int32, (block, block), 0)
     across = lax.broadcasted_iota(jnp.int32, (block, block), 1)
-    pairs = jnp.where(down // phys == across // phys, pairs, 0.0).reshape(group, phys, block).sum(axis=0)
+    same = lax.rem(down, block // 2) // phalf == across // phys
+    pairs = jnp.where(same, pairs, 0.0).reshape(2, group, phalf, block).sum(axis=1).reshape(phys, block)
     tall = lax.broadcasted_iota(jnp.int32, (block, phys), 0)
     wide = lax.broadcasted_iota(jnp.int32, (block, phys), 1)
     fold = jnp.where(lax.rem(tall, phys) == wide, 1.0, 0.0)
@@ -329,8 +334,8 @@
     count, sections = lax.axis_size("cols"), lax.axis_size("rows")
     left_odd = (jnp.arange(bond) >= charge)[None, :, None]
     low, high = stored[:, :, :half], stored[:, :, half:]
-    even = jnp.einsum("pq,qlc->plc", oper[:phalf], jnp.where(left_odd, high, low), preferred_element_type=jnp.float32)
-    other = jnp.einsum("pq,qlc->plc", oper[phalf:], jnp.where(left_odd, low, high), preferred_element_type=jnp.float32)
+    even = jnp.einsum("pq,qlc->lpc", oper[:phalf], jnp.where(left_odd, high, low), preferred_element_type=jnp.float32)
+    other = jnp.einsum("pq,qlc->lpc", oper[phalf:], jnp.where(left_odd, low, high), preferred_element_type=jnp.float32)
     even = even.astype(jnp.bfloat16).reshape(-1, half)
     other = other.astype(jnp.bfloat16).reshape(-1, half)
     scale = 2.0 / (count * phys * bond)
@@ -342,7 +347,7 @@
     compressed, gradient = pl.pallas_call(
         functools.partial(whole_kernel, count, sections, phys, bond, scale, mix_scale),
         out_shape=(
-            jax.ShapeDtypeStruct((phys * bond, bond), jnp.bfloat16),
+            jax.ShapeDtypeStruct((phys, bond, bond), jnp.bfloat16),
             jax.ShapeDtypeStruct((phys, phys), jnp.float32),
         ),
         in_specs=[vmem, vmem, pl.BlockSpec(memory_space=pl.ANY), pl.BlockSpec(memory_space=pltpu.SMEM)],
@@ -354,7 +359,7 @@
             pltpu.VMEM((phys * bond, bond), jnp.bfloat16),
             pltpu.VMEM((bond, phys * bond), jnp.bfloat16),
             pltpu.VMEM((bond, phys * bond), jnp.bfloat16),
-            pltpu.VMEM((phys * bond, bond), jnp.bfloat16),
+            pltpu.VMEM((phys, bond, bond), jnp.bfloat16),
             pltpu.VMEM((8, half), jnp.int32),
             pltpu.VMEM((8, half), jnp.int32),
             pltpu.VMEM((2, half, half), jnp.float32),

time: 63.2 us -> 63.5 us (level)
  local copies, waits for them, and re-layouts: 5.48 us -> 3.71 us
  matrix products: 1.33 us -> 2.93 us
    convert_element_type x2 -> x0, local copies, waits for them, and re-layouts: 1.77 us -> none  [the longest x1 0.89 us: shards(): even = even.astype(jnp.bfloat16).reshape(-1, half)]
    dot_general x2, matrix products: 1.33 us -> 2.93 us  [the longest x1 1.47 us: shards(): jnp.einsum('pq,qlc->lpc', oper[phalf:], jnp.where(left_odd, low, high), p...]
where the time goes in v5:
time: 63.5 us; the launch traced here: 63 us
  Pallas kernels  53.3 us (84%)
  local copies, waits for them, and re-layouts  3.71 us (6%)
  matrix products  2.93 us (5%)
  other arithmetic  1.77 us (3%)
  between operations  1.32 us (2%)
    pallas_call x1, Pallas kernels, shards(): pl.pallas_call(functools.partial(whole_kernel, count, sections, phys, bon...  53.3 us
    unnamed x6, local copies, waits for them, and re-layouts  3.71 us
    select_n x1, other arithmetic, shards(): jnp.where(left_odd, low, high)  1.76 us
    dot_general x1, matrix products, shards(): jnp.einsum('pq,qlc->lpc', oper[phalf:], jnp.where(left_odd, low, high), p...  1.47 us
    dot_general x1, matrix products, shards(): jnp.einsum('pq,qlc->lpc', oper[:phalf], jnp.where(left_odd, high, low), p...  1.46 us

profile of v5, /device:TPU:1, one launch (start us, length us, event | category | flops | bytes accessed | tf_op | source)
XLA Modules:
  0.0 63.0 jit_solution(13100619711856110108)
XLA Ops:
  1.3 0.0 copy-start.1
  1.3 1.8 %broadcast_select_fusion = (bf16[16,256,128]{2,1,0:T(8,128)(2,1)S(1)}, bf16[16,256,128]{2,1,0:T(8,128)(2,1)S(1)}) fusion(pred[256]{0:T(512)(128)(4,1)S(1)} %iota_compare_fusion, bf16[16,256,256]{2,1,0:T(8,128)(2,1)} %bitcast.23), kind=kLoop, calls=%fused_computation.6 | loop fusion | flops 1048576 | bytes 4194560 | tf_op jit(solution)/shard_map/jit(_where)/select_n | solution.py:338
  3.1 0.0 copy-done.1
  3.1 1.5 %fusion.other_ref = bf16[2048,128]{1,0:T(8,128)(2,1)} fusion(bf16[16,256,128]{2,1,0:T(8,128)(2,1)S(1)} %get-tuple-element.6, bf16[1,1,16,16]{3,2,1,0:T(8,128)(2,1)S(1)} %copy-done.1), kind=kOutput, calls=%fused_computation.1 | convolution fusion | flops 8650752 | bytes 1574912 | tf_op jit(solution)/shard_map/pq,qlc->lpc/dot_general | solution.py:338
  4.6 1.5 %fusion.1.even_ref = bf16[2048,128]{1,0:T(8,128)(2,1)} fusion(bf16[16,256,128]{2,1,0:T(8,128)(2,1)S(1)} %get-tuple-element.7, bf16[1,1,16,16]{3,2,1,0:T(8,128)(2,1)S(1)} %copy-done.1), kind=kOutput, calls=%fused_computation.3 | convolution fusion | flops 8650752 | bytes 1574912 | tf_op jit(solution)/shard_map/pq,qlc->lpc/dot_general | solution.py:337
  6.0 53.3 %orthonormalise.1 = (bf16[16,256,256]{2,1,0:T(8,128)(2,1)}, f32[16,16]{1,0:T(8,128)}) custom-call(bf16[2048,128]{1,0:T(8,128)(2,1)} %fusion.1.even_ref, bf16[2048,128]{1,0:T(8,128)(2,1)} %fusion.other_ref, bf16[16,256,256]{2,1,0:T(8,128)(2,1)} %bitcast.24, s32[1,1]{1,0:T(1,128)} %copy.13.charge_ref), custom_call_target="tpu_custom_call" | custom-call | tf_op jit(solution)/shard_map/orthonormalise/pallas_call | solution.py:347
  59.3 0.0 copy-start
  59.3 3.1 %copy.14 = bf16[1,1,16,256,256]{4,3,2,1,0:T(8,128)(2,1)} copy(bf16[1,1,16,256,256]{4,3,2,1,0:T(8,128)(2,1)} %bitcast.25) | data formatting | bytes 4194304
  62.4 0.0 copy-done
  62.4 0.6 copy.15
  (1 shorter events, 0.0 us)
Async XLA Ops:
  1.3 1.8 %copy-start.1 = (bf16[1,1,16,16]{3,2,1,0:T(8,128)(2,1)S(1)}, bf16[1,1,16,16]{3,2,1,0:T(8,128)(2,1)}, u32[]{:S(2)}) copy-start(bf16[1,1,16,16]{3,2,1,0:T(8,128)(2,1)} %param.4) | copy-start | bytes 1540
  59.3 3.1 %copy-start = (f32[16,16]{1,0:T(8,128)S(1)}, f32[16,16]{1,0:T(8,128)}, u32[]{:S(2)}) copy-start(f32[16,16]{1,0:T(8,128)} %get-tuple-element.5) | copy-start | bytes 3076

commit v6 on v5

--- a/solution.py
+++ b/solution.py
@@ -74,6 +74,17 @@
     return jnp.concatenate([jnp.where(odd, 0.0, out[:, :half]), jnp.where(odd, out[:, half:], 0.0)], axis=1).astype(jnp.bfloat16)
 
 
+def spread_kernel(steps, charge_ref, rows_ref, pairs_ref, out_ref, grad_ref):
+    half = rows_ref.shape[2]
+    phys_odd = (pl.program_id(0) >= steps).astype(jnp.int32)
+    left_odd = (lax.broadcasted_iota(jnp.int32, rows_ref.shape, 1) >= charge_ref[0, 0]).astype(jnp.int32)
+    odd = left_odd != phys_odd
+    rows = rows_ref[...].astype(jnp.float32)
+    out_ref[:, :, :half] = jnp.where(odd, 0.0, rows).astype(jnp.bfloat16)
+    out_ref[:, :, half:] = jnp.where(odd, rows, 0.0).astype(jnp.bfloat16)
+    grad_ref[...] = pairs_ref[...]
+
+
 def whole_kernel(
     count, sections, phys, bond, scale, mix_scale,
     even_ref, other_ref, stored_hbm, charge_ref,
@@ -214,6 +225,18 @@
     invert_factor(state, half, 0, half)
     inverse_down = to_below(state, inverse_next, pieces + 1)
     inverse_down.start()
+    own = exact_parts(jnp.concatenate([state[0].T, state[1].T], axis=1))
+
+    def compress_half(which):
+        @pl.loop(0, per_half)
+        def _(step):
+            wide = exact_dot(packed[which][rows_of(step), :], own)
+            wide = jnp.where(odd_rows(which, step, charge), wide[:, half:], wide[:, :half])
+            wide = jnp.swapaxes(wide.reshape(lefts, phalf, half), 0, 1)
+            left = pl.ds(pl.multiple_of(step * lefts, lefts), lefts)
+            out[which * phalf : (which + 1) * phalf, left, :] = wide.astype(jnp.bfloat16)
+
+    compress_half(0)
     charge_down.wait_recv()
     charge_above = charge_next[0:1, :]
     cross = jnp.zeros((bond, bond), jnp.float32)
@@ -236,17 +259,7 @@
         scatter(k, cross_part, cross_land, send_c, recv_c).start()
 
     cross_land[0] = cross_part[me]
-    own = exact_parts(jnp.concatenate([state[0].T, state[1].T], axis=1))
-    for which in range(2):
-
-        @pl.loop(0, per_half)
-        def _(step, which=which):
-            wide = exact_dot(packed[which][rows_of(step), :], own)
-            wide = mask_halves(wide, odd_rows(which, step, charge)).astype(jnp.float32)
-            wide = jnp.swapaxes(wide.reshape(lefts, phalf, bond), 0, 1)
-            left = pl.ds(pl.multiple_of(step * lefts, lefts), lefts)
-            out[which * phalf : (which + 1) * phalf, left, :] = wide.astype(jnp.bfloat16)
-
+    compress_half(1)
     store = pltpu.make_async_copy(out, out_hbm, store_sem)
     store.start()
 
@@ -347,7 +360,7 @@
     compressed, gradient = pl.pallas_call(
         functools.partial(whole_kernel, count, sections, phys, bond, scale, mix_scale),
         out_shape=(
-            jax.ShapeDtypeStruct((phys, bond, bond), jnp.bfloat16),
+            jax.ShapeDtypeStruct((phys, bond, half), jnp.bfloat16),
             jax.ShapeDtypeStruct((phys, phys), jnp.float32),
         ),
         in_specs=[vmem, vmem, pl.BlockSpec(memory_space=pl.ANY), pl.BlockSpec(memory_space=pltpu.SMEM)],
@@ -359,7 +372,7 @@
             pltpu.VMEM((phys * bond, bond), jnp.bfloat16),
             pltpu.VMEM((bond, phys * bond), jnp.bfloat16),
             pltpu.VMEM((bond, phys * bond), jnp.bfloat16),
-            pltpu.VMEM((phys, bond, bond), jnp.bfloat16),
+            pltpu.VMEM((phys, bond, half), jnp.bfloat16),
             pltpu.VMEM((8, half), jnp.int32),
             pltpu.VMEM((8, half), jnp.int32),
             pltpu.VMEM((2, half, half), jnp.float32),
@@ -379,6 +392,25 @@
         compiler_params=pltpu.CompilerParams(collective_id=0, has_side_effects=True),
         name="orthonormalise",
     )(even, other, stored, charges)
+    spread = 4
+    compressed, gradient = pl.pallas_call(
+        functools.partial(spread_kernel, phalf // spread),
+        grid=(phys // spread,),
+        out_shape=(
+            jax.ShapeDtypeStruct((phys, bond, bond), jnp.bfloat16),
+            jax.ShapeDtypeStruct((phys, phys), jnp.float32),
+        ),
+        in_specs=[
+            pl.BlockSpec(memory_space=pltpu.SMEM),
+            pl.BlockSpec((spread, bond, half), lambda i: (i, 0, 0)),
+            pl.BlockSpec((phys, phys), lambda i: (0, 0)),
+        ],
+        out_specs=(
+            pl.BlockSpec((spread, bond, bond), lambda i: (i, 0, 0)),
+            pl.BlockSpec((phys, phys), lambda i: (0, 0)),
+        ),
+        name="spread",
+    )(charges, compressed, gradient)
     return (compressed.reshape(boundary_in.shape), gradient[None, None])
 
 

time: 63.5 us -> 64.7 us (1.019)
  Pallas kernels: 53.3 us -> 58.4 us
  local copies, waits for them, and re-layouts: 3.71 us -> 0.01 us
    pallas_call x0 -> x1, Pallas kernels: none -> 3.82 us  [shards(): pl.pallas_call(functools.partial(spread_kernel, phalf // spread), grid=(p...]
    unnamed x6 -> x2, local copies, waits for them, and re-layouts: 3.71 us -> 0.01 us
    pallas_call x1, Pallas kernels: 53.3 us -> 54.6 us  [shards(): pl.pallas_call(functools.partial(whole_kernel, count, sections, phys, bon...]
where the time goes in v6:
time: 64.7 us; the launch traced here: 64.4 us
  Pallas kernels  58.4 us (90%)
  matrix products  2.95 us (5%)
  other arithmetic  1.77 us (3%)
  between operations  1.32 us (2%)
    pallas_call x1, Pallas kernels, shards(): pl.pallas_call(functools.partial(whole_kernel, count, sections, phys, bon...  54.6 us
    pallas_call x1, Pallas kernels, shards(): pl.pallas_call(functools.partial(spread_kernel, phalf // spread), grid=(p...  3.82 us
    select_n x1, other arithmetic, shards(): jnp.where(left_odd, low, high)  1.76 us
    dot_general x1, matrix products, shards(): jnp.einsum('pq,qlc->lpc', oper[phalf:], jnp.where(left_odd, low, high), p...  1.48 us
    dot_general x1, matrix products, shards(): jnp.einsum('pq,qlc->lpc', oper[:phalf], jnp.where(left_odd, high, low), p...  1.46 us

profile of v6, /device:TPU:1, one launch (start us, length us, event | category | flops | bytes accessed | tf_op | source)
XLA Modules:
  0.0 64.4 jit_solution(1869541497792974903)
XLA Ops:
  1.3 0.0 copy-start
  1.3 1.8 %broadcast_select_fusion = (bf16[16,256,128]{2,1,0:T(8,128)(2,1)S(1)}, bf16[16,256,128]{2,1,0:T(8,128)(2,1)S(1)}) fusion(pred[256]{0:T(512)(128)(4,1)S(1)} %iota_compare_fusion, bf16[16,256,256]{2,1,0:T(8,128)(2,1)} %bitcast.23), kind=kLoop, calls=%fused_computation.6 | loop fusion | flops 1048576 | bytes 4194560 | tf_op jit(solution)/shard_map/jit(_where)/select_n | solution.py:351
  3.1 0.0 copy-done
  3.1 1.5 %fusion.other_ref = bf16[2048,128]{1,0:T(8,128)(2,1)} fusion(bf16[16,256,128]{2,1,0:T(8,128)(2,1)S(1)} %get-tuple-element.10, bf16[1,1,16,16]{3,2,1,0:T(8,128)(2,1)S(1)} %copy-done), kind=kOutput, calls=%fused_computation.1 | convolution fusion | flops 8650752 | bytes 1574912 | tf_op jit(solution)/shard_map/pq,qlc->lpc/dot_general | solution.py:351
  4.6 1.5 %fusion.1.even_ref = bf16[2048,128]{1,0:T(8,128)(2,1)} fusion(bf16[16,256,128]{2,1,0:T(8,128)(2,1)S(1)} %get-tuple-element.11, bf16[1,1,16,16]{3,2,1,0:T(8,128)(2,1)S(1)} %copy-done), kind=kOutput, calls=%fused_computation.3 | convolution fusion | flops 8650752 | bytes 1574912 | tf_op jit(solution)/shard_map/pq,qlc->lpc/dot_general | solution.py:350
  6.0 54.6 %orthonormalise.1 = (bf16[16,256,128]{2,1,0:T(8,128)(2,1)}, f32[16,16]{1,0:T(8,128)}) custom-call(bf16[2048,128]{1,0:T(8,128)(2,1)} %fusion.1.even_ref, bf16[2048,128]{1,0:T(8,128)(2,1)} %fusion.other_ref, bf16[16,256,256]{2,1,0:T(8,128)(2,1)} %bitcast.24, s32[1,1]{1,0:T(1,128)} %copy.11.charge_ref), custom_call_target="tpu_custom_call" | custom-call | tf_op jit(solution)/shard_map/orthonormalise/pallas_call | solution.py:360
  60.6 3.8 %spread.1 = (bf16[16,256,256]{2,1,0:T(8,128)(2,1)}, f32[16,16]{1,0:T(8,128)}) custom-call(s32[1,1]{1,0:T(1,128)} %copy.11.charge_ref, bf16[16,256,128]{2,1,0:T(8,128)(2,1)} %get-tuple-element.6.rows_ref, f32[16,16]{1,0:T(8,128)} %get-tuple-element.7.pairs_ref), custom_call_target="tpu_custom_call" | custom-call | tf_op jit(solution)/shard_map/spread/pallas_call | solution.py:396
  (1 shorter events, 0.0 us)
Async XLA Ops:
  1.3 1.8 %copy-start = (bf16[1,1,16,16]{3,2,1,0:T(8,128)(2,1)S(1)}, bf16[1,1,16,16]{3,2,1,0:T(8,128)(2,1)}, u32[]{:S(2)}) copy-start(bf16[1,1,16,16]{3,2,1,0:T(8,128)(2,1)} %param.4) | copy-start | bytes 1540

commit v7 on v5

--- a/solution.py
+++ b/solution.py
@@ -98,7 +98,7 @@
     pl.semaphore_signal(barrier, inc=1, device_id={"rows": below}, device_id_type=MESH)
     pl.semaphore_signal(barrier, inc=1, device_id={"rows": above}, device_id_type=MESH)
 
-    @pl.loop(1, count)
+    @pl.loop(1, count, unroll=True)
     def _(k):
         pl.semaphore_signal(barrier, inc=1, device_id={"cols": after(k)}, device_id_type=MESH)
 
@@ -231,7 +231,7 @@
     cross_part[: count // 2] = cross[:, :half].reshape(count // 2, -1, half)
     cross_part[count // 2 :] = cross[:, half:].reshape(count // 2, -1, half)
 
-    @pl.loop(1, count)
+    @pl.loop(1, count, unroll=True)
     def _(k):
         scatter(k, cross_part, cross_land, send_c, recv_c).start()
 
@@ -250,13 +250,13 @@
     store = pltpu.make_async_copy(out, out_hbm, store_sem)
     store.start()
 
-    @pl.loop(1, count)
+    @pl.loop(1, count, unroll=True)
     def _(k):
         scatter(k, cross_part, cross_land, send_c, recv_c).wait_recv()
 
     cross_all[me] = jnp.sum(cross_land[...], axis=0)
 
-    @pl.loop(1, count)
+    @pl.loop(1, count, unroll=True)
     def _(k):
         gather(k, me, cross_all, send_d, recv_d).start()
 
@@ -271,6 +271,12 @@
             compressed_next[rows, :] = mask_halves(wide, odd_rows(which, step, charge_above))
 
     @pl.loop(1, count)
+    def _(k):
+        scatter(k, gram_part, gram_land, send_a, recv_a).wait_send()
+        gather(k, me, gram_all, send_b, recv_b).wait_send()
+        scatter(k, cross_part, cross_land, send_c, recv_c).wait_send()
+
+    @pl.loop(1, count, unroll=True)
     def _(k):
         gather(k, before(k), cross_all, send_d, recv_d).wait_recv()
 
@@ -319,11 +325,8 @@
     inverse_down.wait_send()
     store.wait()
 
-    @pl.loop(1, count)
-    def _(k):
-        scatter(k, gram_part, gram_land, send_a, recv_a).wait_send()
-        gather(k, me, gram_all, send_b, recv_b).wait_send()
-        scatter(k, cross_part, cross_land, send_c, recv_c).wait_send()
+    @pl.loop(1, count, unroll=True)
+    def _(k):
         gather(k, me, cross_all, send_d, recv_d).wait_send()
 
 

time: 63.5 us -> 63.1 us (level)
  no operation moved by 1% of the time
where the time goes in v7:
time: 63.1 us; the launch traced here: 62.6 us
  Pallas kernels  52.8 us (84%)
  local copies, waits for them, and re-layouts  3.71 us (6%)
  matrix products  2.93 us (5%)
  other arithmetic  1.77 us (3%)
  between operations  1.32 us (2%)
    pallas_call x1, Pallas kernels, shards(): pl.pallas_call(functools.partial(whole_kernel, count, sections, phys, bon...  52.8 us
    unnamed x6, local copies, waits for them, and re-layouts  3.71 us
    select_n x1, other arithmetic, shards(): jnp.where(left_odd, low, high)  1.76 us
    dot_general x1, matrix products, shards(): jnp.einsum('pq,qlc->lpc', oper[phalf:], jnp.where(left_odd, low, high), p...  1.47 us
    dot_general x1, matrix products, shards(): jnp.einsum('pq,qlc->lpc', oper[:phalf], jnp.where(left_odd, high, low), p...  1.46 us

profile of v7, /device:TPU:1, one launch (start us, length us, event | category | flops | bytes accessed | tf_op | source)
XLA Modules:
  0.0 62.6 jit_solution(2640136252524648408)
XLA Ops:
  1.3 0.0 copy-start.1
  1.3 1.8 %broadcast_select_fusion = (bf16[16,256,128]{2,1,0:T(8,128)(2,1)S(1)}, bf16[16,256,128]{2,1,0:T(8,128)(2,1)S(1)}) fusion(pred[256]{0:T(512)(128)(4,1)S(1)} %iota_compare_fusion, bf16[16,256,256]{2,1,0:T(8,128)(2,1)} %bitcast.23), kind=kLoop, calls=%fused_computation.6 | loop fusion | flops 1048576 | bytes 4194560 | tf_op jit(solution)/shard_map/jit(_where)/select_n | solution.py:341
  3.1 0.0 copy-done.1
  3.1 1.5 %fusion.other_ref = bf16[2048,128]{1,0:T(8,128)(2,1)} fusion(bf16[16,256,128]{2,1,0:T(8,128)(2,1)S(1)} %get-tuple-element.6, bf16[1,1,16,16]{3,2,1,0:T(8,128)(2,1)S(1)} %copy-done.1), kind=kOutput, calls=%fused_computation.1 | convolution fusion | flops 8650752 | bytes 1574912 | tf_op jit(solution)/shard_map/pq,qlc->lpc/dot_general | solution.py:341
  4.6 1.5 %fusion.1.even_ref = bf16[2048,128]{1,0:T(8,128)(2,1)} fusion(bf16[16,256,128]{2,1,0:T(8,128)(2,1)S(1)} %get-tuple-element.7, bf16[1,1,16,16]{3,2,1,0:T(8,128)(2,1)S(1)} %copy-done.1), kind=kOutput, calls=%fused_computation.3 | convolution fusion | flops 8650752 | bytes 1574912 | tf_op jit(solution)/shard_map/pq,qlc->lpc/dot_general | solution.py:340
  6.0 52.8 %orthonormalise.1 = (bf16[16,256,256]{2,1,0:T(8,128)(2,1)}, f32[16,16]{1,0:T(8,128)}) custom-call(bf16[2048,128]{1,0:T(8,128)(2,1)} %fusion.1.even_ref, bf16[2048,128]{1,0:T(8,128)(2,1)} %fusion.other_ref, bf16[16,256,256]{2,1,0:T(8,128)(2,1)} %bitcast.24, s32[1,1]{1,0:T(1,128)} %copy.13.charge_ref), custom_call_target="tpu_custom_call" | custom-call | tf_op jit(solution)/shard_map/orthonormalise/pallas_call | solution.py:350
  58.8 0.0 copy-start
  58.9 3.1 %copy.14 = bf16[1,1,16,256,256]{4,3,2,1,0:T(8,128)(2,1)} copy(bf16[1,1,16,256,256]{4,3,2,1,0:T(8,128)(2,1)} %bitcast.25) | data formatting | bytes 4194304
  62.0 0.0 copy-done
  62.0 0.6 copy.15
  (1 shorter events, 0.0 us)
Async XLA Ops:
  1.3 1.8 %copy-start.1 = (bf16[1,1,16,16]{3,2,1,0:T(8,128)(2,1)S(1)}, bf16[1,1,16,16]{3,2,1,0:T(8,128)(2,1)}, u32[]{:S(2)}) copy-start(bf16[1,1,16,16]{3,2,1,0:T(8,128)(2,1)} %param.4) | copy-start | bytes 1540
  58.8 3.1 %copy-start = (f32[16,16]{1,0:T(8,128)S(1)}, f32[16,16]{1,0:T(8,128)}, u32[]{:S(2)}) copy-start(f32[16,16]{1,0:T(8,128)} %get-tuple-element.5) | copy-start | bytes 3076
